TPU v7x, 32 devices: a whole 2x2x4 slice. The times are simulated.
32 devices in a mesh: copy: 2 (over y), grid: 4 (over z), blk: 2 (over x), sub: 2 (over core).
Axes of the slice: x: 2, y: 2, z: 4, core: 2. Of those that a mesh axis runs over, the one named last changes fastest.
Arguments:
- ensemble: float32 [128, 3, 256, 1024], P(('copy', 'grid'), None, 'blk', 'sub'), parts along dimension 0, may hold values from -6 to 6
- basin_thickness: float32 [512, 1024], P(('copy', 'blk'), 'sub'), parts along dimension 0, may hold values from 0.25 to 2
- wet_indicator: int32 [512, 1024], P(('copy', 'blk'), 'sub'), parts along dimension 0, may hold values 0 or 1
- obs_cell: int32 [4, 4, 2, 64], P(('copy', 'blk'), 'grid', 'sub'), parts along dimension 0, may hold values from 0 to 16383
- obs_count: int32 [4, 4, 2], P(('copy', 'blk'), 'grid', 'sub'), parts along dimension 0, may hold values from 16 to 64, as said below
- obs_value: float32 [4, 4, 2, 64], P(('copy', 'blk'), 'grid', 'sub'), parts along dimension 0, may hold values from -6 to 6
- obs_error: float32 [4, 4, 2, 64], P(('copy', 'blk'), 'grid', 'sub'), parts along dimension 0, may hold values from 0.5 to 2
Outputs:
- analysis: float32 [128, 3, 2, 128, 1024], P('copy', None, 'blk', 'grid', 'sub'), parts along dimension 0
There are 2 independent parts, one for each index of `copy`. A program takes and returns all parts, laid end to end along the dimension named above; each array names one. Nothing has to cross between parts.
Inputs may be any that keep to these rules, and one draw needn't show every extreme that they name: `obs_count`: one block of every draw has all 64 slots live.
All inputs are finite; a program needn't handle non-finite values. No bound on the sum of `wet_indicator` on one device may be relied on, other than what follows from the above.
Results may differ from a plain program's by a relative error of at most 0.0003.
Values sent between devices are 32-bit elements; how exact they have to be, the bound alone decides.
No kernel may reach another device: no remote copies, remote signals or barrier semaphores. Data moves between devices by JAX's collectives and lax.ppermute only.
A program may use at most 128 MiB of HBM per device.

v0:
```python
import math

import jax
import jax.numpy as jnp
from jax import lax
from jax.sharding import PartitionSpec as P

STEPS = 2
NS_STEPS = 8


FRICTION = 0.05
PRESSURE = 0.35
DIVERGE = 0.35
CORIOLIS = 0.2
precise = lax.Precision.HIGHEST


def padded(cells, sides, width):
    for axis, dim in sides:
        count = lax.axis_size(axis)
        ends = count - 1
        head = lax.slice_in_dim(cells, 0, width, axis=dim)
        tail = lax.slice_in_dim(cells, cells.shape[dim] - width, cells.shape[dim], axis=dim)
        cells = jnp.concatenate(
            [
                lax.ppermute(tail, axis, [(i, (i + 1) % count) for i in range(ends)]),
                cells,
                lax.ppermute(head, axis, [((i + 1) % count, i) for i in range(ends)]),
            ],
            axis=dim,
        )
    return cells


def thin_step(dynamic_vector, static_local, inner_cor):
    height = dynamic_vector[:, 0]
    bordered_array = padded(height, (("blk", 1), ("sub", 2)), 1)
    inner_depth = static_local[0]
    interior_indicator = static_local[1]
    grad_first = bordered_array[:, 2:, 1:-1] - bordered_array[:, :-2, 1:-1]
    grad_second = bordered_array[:, 1:-1, 2:] - bordered_array[:, 1:-1, :-2]
    first_new = interior_indicator * (
        (1.0 - FRICTION) * dynamic_vector[:, 1]
        + inner_cor * dynamic_vector[:, 2]
        - PRESSURE * grad_first
    )
    second_new = interior_indicator * (
        (1.0 - FRICTION) * dynamic_vector[:, 2]
        - inner_cor * dynamic_vector[:, 1]
        - PRESSURE * grad_second
    )
    fluxes = jnp.stack([inner_depth * first_new, inner_depth * second_new], axis=1)
    flux_wide = padded(fluxes, (("blk", 2), ("sub", 3)), 1)
    divergence = (
        flux_wide[:, 0, 2:, 1:-1]
        - flux_wide[:, 0, :-2, 1:-1]
        + (flux_wide[:, 1, 1:-1, 2:] - flux_wide[:, 1, 1:-1, :-2])
    )
    height_new = height - DIVERGE * divergence
    return jnp.stack([height_new, first_new, second_new], axis=1)


def observe(surface_height, obs_cell, obs_count, obs_value, obs_error):
    members = surface_height.shape[0]
    flat = surface_height.reshape(members, -1)
    cells = obs_cell.reshape(-1)
    picked = jnp.take(flat, cells, axis=1)
    pbar = jnp.mean(picked, axis=0)
    valid = jnp.arange(cells.shape[0], dtype=jnp.int32) < obs_count.reshape(())
    scale = jnp.where(valid, 1.0 / (obs_error.reshape(-1) * math.sqrt(members - 1)), 0.0)
    anomobs = (picked - pbar) * scale
    innov = (obs_value.reshape(-1) - pbar) * scale
    gram = jnp.dot(anomobs, anomobs.T, precision=precise)
    proj = jnp.dot(anomobs, innov, precision=precise)
    return jnp.concatenate([gram, proj[None]], axis=0)


def domain_reduction(packed):
    packed = lax.psum(packed, ("blk", "sub"))
    return packed


def transform(packed):
    members = packed.shape[1]
    eye = jnp.eye(members, dtype=jnp.float32)
    system = eye + packed[:members]
    proj = packed[members]
    factor_low = jnp.linalg.cholesky(system)
    mean_w = jax.scipy.linalg.cho_solve((factor_low, True), proj)
    scale = jnp.sqrt(jnp.sum(system * system))
    ystate = system / scale
    zstate = eye
    for sweep in range(NS_STEPS):
        factor = 1.5 * eye - 0.5 * jnp.dot(zstate, ystate, precision=precise)
        ystate = jnp.dot(ystate, factor, precision=precise)
        zstate = jnp.dot(factor, zstate, precision=precise)
    return mean_w[:, None] + zstate / jnp.sqrt(scale)


def shards(ensemble, basin_thickness, wet_indicator, obs_cell, obs_count, obs_value, obs_error):
    rows_dev = ensemble.shape[2]
    constant_fields = jnp.stack([basin_thickness, wet_indicator.astype(jnp.float32)])
    total_rows = rows_dev * lax.axis_size("blk")
    rows = (
        lax.axis_index("blk") * rows_dev + jnp.arange(-2, rows_dev + 2, dtype=jnp.int32)
    ).astype(jnp.float32)
    latitude_coupling = (CORIOLIS * (2.0 * (rows + 0.5) / total_rows - 1.0))[:, None]
    dynamic_vector = ensemble
    inner_cor = latitude_coupling[2:-2]
    for number in range(STEPS):
        dynamic_vector = thin_step(dynamic_vector, constant_fields, inner_cor)
    blocks = lax.all_to_all(dynamic_vector, "grid", split_axis=2, concat_axis=0, tiled=True)
    packed = domain_reduction(observe(blocks[:, 0], obs_cell, obs_count, obs_value, obs_error))
    weights = transform(packed)
    members = blocks.shape[0]
    flat = blocks.reshape(members, -1)
    center = jnp.mean(flat, axis=0)
    member_deviations = flat - center
    updated = center + jnp.dot(weights.T, member_deviations, precision=precise)
    return updated.reshape(members, 3, 1, blocks.shape[2], blocks.shape[3])


def solution(mesh):
    placed = (
        P(("copy", "grid"), None, "blk", "sub"),
        P(("copy", "blk"), "sub"),
        P(("copy", "blk"), "sub"),
        P(("copy", "blk"), "grid", "sub", None),
        P(("copy", "blk"), "grid", "sub"),
        P(("copy", "blk"), "grid", "sub", None),
        P(("copy", "blk"), "grid", "sub", None),
    )
    return jax.shard_map(
        shards,
        mesh=mesh,
        in_specs=placed,
        out_specs=P("copy", None, "blk", "grid", "sub"),
        check_vma=False,
    )
```

profile of v0, /device:TPU:0, one launch (start us, length us, event | category | flops | bytes accessed | tf_op | source)
XLA Modules:
  0.0 581.9 jit_solution(4712304430399835638)
XLA Ops:
  0.0 10.2 %fusion.67 = (f32[16,1,128,512]{3,2,1,0:T(8,128)}, f32[16,1,128,512]{3,2,1,0:T(8,128)}, f32[16,1,128,512]{3,2,1,0:T(8,128)S(1)}) fusion(f32[16,3,128,512]{3,2,1,0:T(8,128)} %param.7), kind=kLoop, calls=%fused_computation.164 | loop fusion | bytes 25165824 | tf_op jit(solution)/shard_map/slice | solution.py:45
  10.2 2.4 copy.107
  12.7 2.0 copy-done.5
  14.7 1.3 collective-permute-start
  15.9 4.8 collective-permute-start.1
  20.8 1.5 collective-permute-done.1
  22.4 1.9 pad_maximum_fusion.54
  24.3 0.7 copy.51
  24.9 1.3 collective-permute-start.2
  26.2 0.7 copy.53
  26.9 3.2 collective-permute-start.3
  30.2 0.8 copy.52
  31.0 0.8 copy.54
  31.8 21.8 %multiply_bitcast_fusion.3 = (f32[16,1,128,512]{3,0,2,1:T(8,128)S(1)}, f32[16,128,512]{2,0,1:T(8,128)}, f32[16,1,128,512]{3,0,2,1:T(8,128)}, f32[16,128,512]{2,0,1:T(8,128)}) fusion(f32[128,512]{1,0:T(8,128)S(1)} %copy-done.8, f32[16,128,512]{2,0,1:T(8,128)} %bitcast.143, f32[16,1,512]{2,0,1:T(8,128)S(1)} %collective-permute-done.1, ...), kind=kLoop, calls=%fused_computation.76 | loop fusion | flops 25165824 | bytes 29967104 | tf_op jit(solution)/shard_map/stack | solution.py:53
  53.6 1.0 pad_maximum_fusion.57
  54.7 1.6 collective-permute-start.4
  56.2 4.7 collective-permute-start.5
  61.2 1.6 collective-permute-done.5
  62.8 2.1 pad_maximum_fusion.48
  64.9 2.8 copy.55
  67.8 1.3 collective-permute-start.6
  69.1 1.9 copy.57
  71.0 3.8 collective-permute-start.7
  74.8 2.2 copy.56
  77.0 2.6 copy.58
  79.6 11.1 %bitcast_subtract_fusion = (f32[16,128,512]{2,0,1:T(8,128)S(1)}, f32[16,1,128,512]{3,0,2,1:T(8,128)}) fusion(f32[16,1,128,512]{3,2,1,0:T(8,128)} %copy-done.4, f32[16,2,1,512]{3,0,2,1:T(8,128)S(1)} %collective-permute-done.4, f32[16,1,128,512]{3,0,2,1:T(8,128)} %get-tuple-element.17, f32[16,1,128,512]{3,0,2,1:T(8,128)} %copy-done.2, ...), kind=kLoop, calls=%fused_computation.72 | loop fusion | flops 17825792 | bytes 21135872 | tf_op jit(solution)/shard_map/sub | solution.py:60
  90.8 1.3 collective-permute-start.8
  92.1 4.5 collective-permute-start.9
  96.7 1.6 collective-permute-done.9
  98.6 0.7 copy.59
  99.3 1.3 collective-permute-start.10
  100.6 0.7 copy.61
  101.3 3.0 collective-permute-start.11
  104.3 0.8 copy.60
  105.1 0.8 copy.62
  105.9 17.2 %multiply_bitcast_fusion.1 = (f32[16,1,128,512]{3,0,2,1:T(8,128)S(1)}, f32[16,128,512]{2,0,1:T(8,128)}, f32[16,1,128,512]{3,0,2,1:T(8,128)S(1)}, f32[16,128,512]{2,0,1:T(8,128)}) fusion(f32[128,512]{1,0:T(8,128)} %param.8, f32[16,128,512]{2,0,1:T(8,128)} %copy-done.6, f32[16,1,512]{2,0,1:T(8,128)S(1)} %collective-permute-done.9, ...), kind=kLoop, calls=%fused_computation.74 | loop fusion | flops 25165824 | bytes 29967104 | tf_op jit(solution)/shard_map/stack | solution.py:53
  123.1 1.3 collective-permute-start.12
  124.4 4.5 collective-permute-start.13
  129.3 1.5 collective-permute-done.13
  130.9 2.2 pad_maximum_fusion.44
  133.1 2.8 copy.63
  135.9 1.7 collective-permute-start.14
  137.6 1.3 copy.65
  138.9 3.0 collective-permute-start.15
  141.9 1.5 copy.64
  143.4 2.7 copy.66
  146.1 13.0 %fusion.5 = f32[16,1,128,512]{3,0,2,1:T(8,128)} fusion(f32[16,2,130,1]{3,0,2,1:T(8,128)} %copy.66, f32[16,2,1,512]{3,0,2,1:T(8,128)S(1)} %collective-permute-done.12, f32[16,2,1,512]{3,0,2,1:T(8,128)S(1)} %collective-permute-done.13, f32[16,1,128,512]{3,0,2,1:T(8,128)} %copy-done.1, f32[16,1,128,512]{3,0,2,1:T(8,128)} %copy-done, ...), kind=kLoop, calls=%fused_computation.9 | loop fusion | flops 18874368 | bytes 21135872 | tf_op jit(solution)/shard_map/sub | solution.py:60
  159.1 9.0 %pad_maximum_fusion = f32[16,3,128,512]{3,0,2,1:T(8,128)} fusion(f32[16,1,128,512]{3,0,2,1:T(8,128)} %bitcast.145, f32[16,1,128,512]{3,0,2,1:T(8,128)S(1)} %bitcast.144, f32[16,1,128,512]{3,0,2,1:T(8,128)} %fusion.5), kind=kLoop, calls=%fused_computation.2 | loop fusion | flops 6291456 | bytes 25165824 | tf_op jit(solution)/shard_map/stack | solution.py:61
  168.1 12.1 %copy.67 = f32[16,3,128,512]{3,0,1,2:T(8,128)} copy(f32[16,3,128,512]{3,0,2,1:T(8,128)} %pad_maximum_fusion) | data formatting | bytes 25165824 | tf_op jit(solution)/shard_map/stack | solution.py:61
  180.2 6.6 %all-to-all-start = ((f32[16,3,128,512]{3,0,1,2:T(8,128)}), f32[16,3,128,512]{3,0,1,2:T(8,128)}, u32[]{:S(2)}, u32[]{:S(2)}) async-start(f32[16,3,128,512]{3,0,1,2:T(8,128)} %copy.67), calls=%async_computation | async-start | bytes 25165824 | tf_op jit(solution)/shard_map/all_to_all | solution.py:113
  187.6 273.5 %all-to-all-done = f32[16,3,128,512]{3,0,1,2:T(8,128)} async-done(((f32[16,3,128,512]{3,0,1,2:T(8,128)}), f32[16,3,128,512]{3,0,1,2:T(8,128)}, u32[]{:S(2)}, u32[]{:S(2)}) %all-to-all-start) | async-done | bytes 12582944 | tf_op jit(solution)/shard_map/all_to_all | solution.py:113
  461.1 16.6 %copy.108 = f32[16,3,4,32,512]{4,3,1,0,2:T(8,128)} copy(f32[16,3,4,32,512]{4,0,1,3,2:T(8,128)} %bitcast.10) | data formatting | bytes 25165824 | tf_op jit(solution)/shard_map/all_to_all | solution.py:113
  477.7 5.0 slice.199
  482.7 6.9 %copy.79 = f32[64,1,32,512]{0,3,2,1:T(8,128)} copy(f32[64,1,32,512]{3,2,1,0:T(8,128)} %slice.199) | data formatting | bytes 8388608
  489.7 4.0 gather_fusion
  494.6 11.5 %psum.7 = f32[65,64]{0,1:T(8,128)S(1)} all-reduce(f32[65,64]{0,1:T(8,128)S(1)} %pad_maximum_fusion.59), channel_id=1, replica_groups=mesh['copy'=2,'grid'=4,'blk'=2,'sub'=2] {'blk','sub'}, use_global_device_ids=true, to_apply=%region_2.3 | all-reduce | flops 4160 | bytes 33280 | tf_op jit(solution)/shard_map/psum | solution.py:80
  506.1 0.6 slice_add_fusion
  511.4 11.1 %bitcast_reduce_fusion = f32[3,32,512]{2,1,0:T(8,128)S(1)} fusion(f32[16,3,4,32,512]{4,0,1,3,2:T(8,128)} %bitcast.10), kind=kLoop, calls=%fused_computation.160 | loop fusion | flops 3096576 | bytes 12779520 | tf_op jit(solution)/shard_map/reduce_sum | solution.py:118
  522.5 5.8 %cholesky.26 = f32[64,64]{1,0:T(8,128)S(1)} custom-call(f32[64,64]{1,0:T(8,128)S(1)} %fusion.39), custom_call_target="Cholesky" | custom-call | tf_op jit(solution)/shard_map/jit(cholesky)/cholesky | solution.py:89
  528.6 0.7 compare_reduce_fusion
  529.9 4.9 custom-call.10
  535.1 12.0 %reshape.118 = f32[64,49152]{1,0:T(8,128)} reshape(f32[4,16,3,32,512]{4,3,2,1,0:T(8,128)} %bitcast.139) | data formatting | bytes 25165824 | tf_op jit(solution)/shard_map/reshape | solution.py:117
  547.5 17.4 %convolution_add_fusion = f32[64,49152]{1,0:T(8,128)} fusion(f32[64,64]{1,0:T(8,128)S(1)} %fusion.28, f32[64,49152]{1,0:T(8,128)} %reshape.118, f32[49152]{0:T(1024)S(1)} %bitcast.147), kind=kOutput, calls=%fused_computation.1 | convolution fusion | flops 2422210560 | bytes 25378816 | tf_op jit(solution)/shard_map/dot_general | solution.py:120
  565.0 16.4 %copy.85 = f32[8,8,96,512]{3,2,1,0:T(8,128)} copy(f32[8,8,96,512]{3,1,2,0:T(8,128)} %bitcast.140) | data formatting | bytes 25165824
  (87 shorter events, 7.6 us)
Async XLA Ops:
  10.2 2.4 copy-start.4
  12.6 2.0 copy-start.5
  14.7 6.2 %collective-permute-start = (f32[16,1,512]{2,0,1:T(8,128)S(1)}, f32[16,1,512]{2,0,1:T(8,128)S(1)}, u32[]{:S(2)}, u32[]{:S(2)}) collective-permute-start(f32[16,1,512]{2,0,1:T(8,128)S(1)} %get-tuple-element.39), channel_id=1, source_target_pairs={{2,0},{3,1},{6,4},{7,5},{10,8},{11,9},{14,12},{15,13},{18,16},{19,... | collective-permute-start | bytes 98312 | tf_op jit(solution)/shard_map/ppermute | solution.py:29
  15.9 6.4 %collective-permute-start.1 = (f32[16,1,512]{2,0,1:T(8,128)S(1)}, f32[16,1,512]{2,0,1:T(8,128)S(1)}, u32[]{:S(2)}, u32[]{:S(2)}) collective-permute-start(f32[16,1,512]{2,0,1:T(8,128)S(1)} %get-tuple-element.38), channel_id=1, source_target_pairs={{0,2},{1,3},{4,6},{5,7},{8,10},{9,11},{12,14},{13,15},{16,18},{17,... | collective-permute-start | bytes 98312 | tf_op jit(solution)/shard_map/ppermute | solution.py:27
  20.8 9.3 %copy-start.9 = (s32[128,512]{1,0:T(8,128)S(1)}, s32[128,512]{1,0:T(8,128)}, u32[]{:S(2)}) copy-start(s32[128,512]{1,0:T(8,128)} %param.9) | copy-start | bytes 786436
  20.8 11.0 %copy-start.8 = (f32[128,512]{1,0:T(8,128)S(1)}, f32[128,512]{1,0:T(8,128)}, u32[]{:S(2)}) copy-start(f32[128,512]{1,0:T(8,128)} %param.8) | copy-start | bytes 786436
  24.9 5.3 collective-permute-start.2
  26.9 4.1 collective-permute-start.3
  53.6 9.2 %copy-start.2 = (f32[16,1,128,512]{3,0,2,1:T(8,128)}, f32[16,1,128,512]{3,0,2,1:T(8,128)S(1)}, u32[]{:S(2)}) copy-start(f32[16,1,128,512]{3,0,2,1:T(8,128)S(1)} %get-tuple-element.11) | copy-start | bytes 12582916
  53.6 9.2 %copy-start.3 = (f32[16,1,128,512]{3,0,2,1:T(8,128)S(1)}, f32[16,1,128,512]{3,0,2,1:T(8,128)}, u32[]{:S(2)}) copy-start(f32[16,1,128,512]{3,0,2,1:T(8,128)} %get-tuple-element.17) | copy-start | bytes 12582916
  54.7 6.6 %collective-permute-start.4 = (f32[16,2,1,512]{3,0,2,1:T(8,128)S(1)}, f32[16,2,1,512]{3,0,2,1:T(8,128)S(1)}, u32[]{:S(2)}, u32[]{:S(2)}) collective-permute-start(f32[16,2,1,512]{3,0,2,1:T(8,128)S(1)} %get-tuple-element.31), channel_id=1, source_target_pairs={{2,0},{3,1},{6,4},{7,5},{10,8},{11,9},{14,12},{15,13},{18,16},{19,... | collective-permute-start | bytes 196616 | tf_op jit(solution)/shard_map/ppermute | solution.py:29
  56.2 6.6 %collective-permute-start.5 = (f32[16,2,1,512]{3,0,2,1:T(8,128)S(1)}, f32[16,2,1,512]{3,0,2,1:T(8,128)S(1)}, u32[]{:S(2)}, u32[]{:S(2)}) collective-permute-start(f32[16,2,1,512]{3,0,2,1:T(8,128)S(1)} %get-tuple-element.30), channel_id=1, source_target_pairs={{0,2},{1,3},{4,6},{5,7},{8,10},{9,11},{12,14},{13,15},{16,18},{17,... | collective-permute-start | bytes 196616 | tf_op jit(solution)/shard_map/ppermute | solution.py:27
  67.8 7.0 %collective-permute-start.6 = (f32[16,2,130,1]{2,0,3,1:T(8,128)S(1)}, f32[16,2,130,1]{2,0,3,1:T(8,128)}, u32[]{:S(2)}, u32[]{:S(2)}) collective-permute-start(f32[16,2,130,1]{2,0,3,1:T(8,128)S(1)} %copy.55), channel_id=1, source_target_pairs={{1,0},{3,2},{5,4},{7,6},{9,8},{11,10},{13,12},{15,14},{17,16},{19,... | collective-permute-start | bytes 49928 | tf_op jit(solution)/shard_map/ppermute | solution.py:29
  71.0 6.0 %collective-permute-start.7 = (f32[16,2,130,1]{2,0,3,1:T(8,128)}, f32[16,2,130,1]{2,0,3,1:T(8,128)S(1)}, u32[]{:S(2)}, u32[]{:S(2)}) collective-permute-start(f32[16,2,130,1]{2,0,3,1:T(8,128)} %copy.57), channel_id=1, source_target_pairs={{0,1},{2,3},{4,5},{6,7},{8,9},{10,11},{12,13},{14,15},{16,17},{18,... | collective-permute-start | bytes 49928 | tf_op jit(solution)/shard_map/ppermute | solution.py:27
  90.8 7.5 %copy-start.6 = (f32[16,128,512]{2,0,1:T(8,128)}, f32[16,128,512]{2,0,1:T(8,128)S(1)}, u32[]{:S(2)}) copy-start(f32[16,128,512]{2,0,1:T(8,128)S(1)} %get-tuple-element.9) | copy-start | bytes 12582916
  90.8 5.9 %collective-permute-start.8 = (f32[16,1,512]{2,0,1:T(8,128)S(1)}, f32[16,1,512]{2,0,1:T(8,128)S(1)}, u32[]{:S(2)}, u32[]{:S(2)}) collective-permute-start(f32[16,1,512]{2,0,1:T(8,128)S(1)} %get-tuple-element.37), channel_id=1, source_target_pairs={{2,0},{3,1},{6,4},{7,5},{10,8},{11,9},{14,12},{15,13},{18,16},{19,... | collective-permute-start | bytes 98312 | tf_op jit(solution)/shard_map/ppermute | solution.py:29
  92.1 6.1 %collective-permute-start.9 = (f32[16,1,512]{2,0,1:T(8,128)S(1)}, f32[16,1,512]{2,0,1:T(8,128)S(1)}, u32[]{:S(2)}, u32[]{:S(2)}) collective-permute-start(f32[16,1,512]{2,0,1:T(8,128)S(1)} %get-tuple-element.36), channel_id=1, source_target_pairs={{0,2},{1,3},{4,6},{5,7},{8,10},{9,11},{12,14},{13,15},{16,18},{17,... | collective-permute-start | bytes 98312 | tf_op jit(solution)/shard_map/ppermute | solution.py:27
  99.3 5.0 collective-permute-start.10
  101.3 3.9 collective-permute-start.11
  123.1 7.8 %copy-start = (f32[16,1,128,512]{3,0,2,1:T(8,128)}, f32[16,1,128,512]{3,0,2,1:T(8,128)S(1)}, u32[]{:S(2)}) copy-start(f32[16,1,128,512]{3,0,2,1:T(8,128)S(1)} %get-tuple-element.5) | copy-start | bytes 12582916
  123.1 7.8 %copy-start.1 = (f32[16,1,128,512]{3,0,2,1:T(8,128)}, f32[16,1,128,512]{3,0,2,1:T(8,128)S(1)}, u32[]{:S(2)}) copy-start(f32[16,1,128,512]{3,0,2,1:T(8,128)S(1)} %get-tuple-element.15) | copy-start | bytes 12582916
  123.1 6.2 %collective-permute-start.12 = (f32[16,2,1,512]{3,0,2,1:T(8,128)S(1)}, f32[16,2,1,512]{3,0,2,1:T(8,128)S(1)}, u32[]{:S(2)}, u32[]{:S(2)}) collective-permute-start(f32[16,2,1,512]{3,0,2,1:T(8,128)S(1)} %get-tuple-element.29), channel_id=1, source_target_pairs={{2,0},{3,1},{6,4},{7,5},{10,8},{11,9},{14,12},{15,13},{18,16},{19,... | collective-permute-start | bytes 196616 | tf_op jit(solution)/shard_map/ppermute | solution.py:29
  124.4 6.4 %collective-permute-start.13 = (f32[16,2,1,512]{3,0,2,1:T(8,128)S(1)}, f32[16,2,1,512]{3,0,2,1:T(8,128)S(1)}, u32[]{:S(2)}, u32[]{:S(2)}) collective-permute-start(f32[16,2,1,512]{3,0,2,1:T(8,128)S(1)} %get-tuple-element.28), channel_id=1, source_target_pairs={{0,2},{1,3},{4,6},{5,7},{8,10},{9,11},{12,14},{13,15},{16,18},{17,... | collective-permute-start | bytes 196616 | tf_op jit(solution)/shard_map/ppermute | solution.py:27
  135.9 6.0 %collective-permute-start.14 = (f32[16,2,130,1]{2,0,3,1:T(8,128)S(1)}, f32[16,2,130,1]{2,0,3,1:T(8,128)S(1)}, u32[]{:S(2)}, u32[]{:S(2)}) collective-permute-start(f32[16,2,130,1]{2,0,3,1:T(8,128)S(1)} %copy.63), channel_id=1, source_target_pairs={{1,0},{3,2},{5,4},{7,6},{9,8},{11,10},{13,12},{15,14},{17,16},{19,... | collective-permute-start | bytes 49928 | tf_op jit(solution)/shard_map/ppermute | solution.py:29
  138.9 4.5 collective-permute-start.15
  146.1 13.0 %copy-start.7 = (f32[16,128,512]{2,0,1:T(8,128)S(1)}, f32[16,128,512]{2,0,1:T(8,128)}, u32[]{:S(2)}) copy-start(f32[16,128,512]{2,0,1:T(8,128)} %get-tuple-element.6) | copy-start | bytes 12582916
  180.2 7.4 %copy-start.11 = (s32[1,1,1,64]{3,2,1,0:T(1,128)S(1)}, s32[1,1,1,64]{3,2,1,0:T(1,128)}, u32[]{:S(2)}) copy-start(s32[1,1,1,64]{3,2,1,0:T(1,128)} %param.10) | copy-start | bytes 772
  180.2 280.9 %all-to-all-start = ((f32[16,3,128,512]{3,0,1,2:T(8,128)}), f32[16,3,128,512]{3,0,1,2:T(8,128)}, u32[]{:S(2)}, u32[]{:S(2)}) async-start(f32[16,3,128,512]{3,0,1,2:T(8,128)} %copy.67), calls=%async_computation | async-start | bytes 25165824 | tf_op jit(solution)/shard_map/all_to_all | solution.py:113
  482.7 11.1 %copy-start.10 = (f32[1,1,1,64]{3,2,1,0:T(1,128)S(1)}, f32[1,1,1,64]{3,2,1,0:T(1,128)}, u32[]{:S(2)}) copy-start(f32[1,1,1,64]{3,2,1,0:T(1,128)} %param.13) | copy-start | bytes 772
  482.7 11.5 %copy-start.12 = (f32[1,1,1,64]{3,2,1,0:T(1,128)S(1)}, f32[1,1,1,64]{3,2,1,0:T(1,128)}, u32[]{:S(2)}) copy-start(f32[1,1,1,64]{3,2,1,0:T(1,128)} %param.12) | copy-start | bytes 772
where the time goes:
time: 588 us; the launch traced here: 582 us
  waiting for transfers between devices  280 us (48%)
  local copies, waits for them, and re-layouts  112 us (19%)
  other arithmetic  104 us (18%)
  starting transfers between devices  49.3 us (8%)
  matrix products  22.2 us (4%)
  blocking collectives  11.5 us (2%)
    all_to_all x1, waiting for transfers between devices, shards(): lax.all_to_all(dynamic_vector, 'grid', split_axis=2, concat_axis=0, tiled...  273 us
    another operation x4, other arithmetic, thin_step(): jnp.stack([inner_depth * first_new, inner_depth * second_new], axis=1)  40 us
    ppermute x8, starting transfers between devices, padded(): lax.ppermute(tail, axis, [(i, (i + 1) % count) for i in range(ends)])  31.7 us
    unnamed x30, local copies, waits for them, and re-layouts  27.9 us
    sub x2, other arithmetic, thin_step(): height_new = height - DIVERGE * divergence  24.1 us
    dot_general x1, matrix products, shards(): updated = center + jnp.dot(weights.T, member_deviations, precision=precise)  17.4 us
    all_to_all x1, local copies, waits for them, and re-layouts, shards(): lax.all_to_all(dynamic_vector, 'grid', split_axis=2, concat_axis=0, tiled...  16.6 us
    another operation x1, local copies, waits for them, and re-layouts, thin_step(): return jnp.stack([height_new, first_new, second_new], axis=1)  12.1 us
  transfers between devices with their start and end apart: 17, of which 7 were waited for; matrix products, arithmetic and copies ran while one was open for 2% of the time, Pallas kernels for 0%

commit v1 on v0

v1 whole, which is shorter than its diff:
```python
import functools
import math

import jax
import jax.numpy as jnp
from jax import lax
from jax.experimental import pallas as pl
from jax.experimental.pallas import tpu as pltpu
from jax.sharding import PartitionSpec as P

STEPS = 2
NS_STEPS = 8
FRICTION = 0.05
PRESSURE = 0.35
DIVERGE = 0.35
CORIOLIS = 0.2
HALO = 2 * STEPS
PAD = 8
LANES = 128
f32 = jnp.float32


def thirds(x):
    top = x.astype(jnp.bfloat16)
    x = x - top.astype(f32)
    middle = x.astype(jnp.bfloat16)
    return top, middle, (x - middle.astype(f32)).astype(jnp.bfloat16)


def product(a, b, dims):
    dot = lambda x, y: lax.dot_general(x, y, (dims, ((), ())), preferred_element_type=f32)
    if a.dtype == jnp.bfloat16:
        return dot(a, b)
    (a0, a1, a2), (b0, b1, b2) = thirds(a), thirds(b)
    return ((dot(a2, b0) + dot(a0, b2)) + dot(a1, b1)) + (dot(a1, b0) + dot(a0, b1)) + dot(a0, b0)


def nt(a, b):
    return product(a, b, ((1,), (1,)))


def nn(a, b):
    return product(a, b, ((1,), (0,)))


def pack_kernel(*refs, members, two, statics):
    ens_head, ens_tail, ens_first, ens_last, ens_hf, ens_hl, ens_tf, ens_tl = refs[:8]
    refs = refs[8:]
    if statics:
        thick, wet = refs[:2]
        refs = refs[2:]
    outs = refs
    b, s = lax.axis_index("blk"), lax.axis_index("sub")
    step = pl.program_id(0)

    def emit(head, tail, first, last, corner_head, corner_tail, index):
        if two:
            outs[0][0, index] = jnp.where(b == 0, tail, head)
            outs[1][0, index] = jnp.where(b == 0, corner_tail, corner_head)
        else:
            outs[0][0, index] = head
            outs[1][0, index] = corner_head
            outs[2][0, index] = tail
            outs[3][0, index] = corner_tail
        outs[-1][0, index] = jnp.where(s == 0, last, first)

    def member():
        for field in range(3):
            emit(
                ens_head[0, field, :HALO],
                ens_tail[0, field, PAD - HALO :],
                ens_first[0, field],
                ens_last[0, field],
                jnp.where(s == 0, ens_hl[0, field, :HALO], ens_hf[0, field, :HALO]),
                jnp.where(s == 0, ens_tl[0, field, PAD - HALO :], ens_tf[0, field, PAD - HALO :]),
                field,
            )

    if not statics:
        member()
        return

    pl.when(step < members)(member)

    @pl.when(step == members)
    def _():
        for index, source in enumerate((thick[...], wet[...].astype(f32))):
            rows, columns = source.shape
            head, tail = source[:HALO], source[rows - HALO :]
            first, last = source[:, :LANES], source[:, columns - LANES :]
            emit(
                head,
                tail,
                first,
                last,
                jnp.where(s == 0, head[:, columns - LANES :], head[:, :LANES]),
                jnp.where(s == 0, tail[:, columns - LANES :], tail[:, :LANES]),
                index,
            )


def edges(ensemble, first, members, statics):
    rows, columns = ensemble.shape[2:]
    two = lax.axis_size("blk") == 2
    held = members + (1 if statics else 0)
    row_end, column_end = rows // PAD - 1, columns // LANES - 1

    def taken(block, r, c):
        return pl.BlockSpec((1, 3) + block, lambda i: (first + jnp.minimum(i, members - 1), 0, r, c))

    in_specs = [
        taken((PAD, columns), 0, 0),
        taken((PAD, columns), row_end, 0),
        taken((rows, LANES), 0, 0),
        taken((rows, LANES), 0, column_end),
        taken((PAD, LANES), 0, 0),
        taken((PAD, LANES), 0, column_end),
        taken((PAD, LANES), row_end, 0),
        taken((PAD, LANES), row_end, column_end),
    ]
    operands = [ensemble] * 8
    if statics:
        in_specs += [pl.BlockSpec((rows, columns), lambda i: (0, 0))] * 2
        operands += list(statics)
    shapes = [(3, HALO, columns), (3, HALO, LANES)] * (1 if two else 2) + [(3, rows, LANES)]
    packed = pl.pallas_call(
        functools.partial(pack_kernel, members=members, two=two, statics=bool(statics)),
        grid=(held,),
        in_specs=in_specs,
        out_specs=[pl.BlockSpec((1,) + s, lambda i: (i, 0, 0, 0)) for s in shapes],
        out_shape=[jax.ShapeDtypeStruct((held,) + s, f32) for s in shapes],
        name="edges",
    )(*operands)
    return halo(packed)


def halo(packed):
    count = lax.axis_size("blk")
    beside = lax.ppermute(packed[-1], "sub", [(0, 1), (1, 0)])
    if count == 2:
        lines = lax.ppermute(packed[0], "blk", [(0, 1), (1, 0)])
        corners = lax.ppermute(packed[1], ("blk", "sub"), [(0, 3), (3, 0), (1, 2), (2, 1)])
        return lines, lines, beside, corners, corners
    up = [(i + 1, i) for i in range(count - 1)]
    down = [(i, i + 1) for i in range(count - 1)]
    below = lax.ppermute(packed[0], "blk", up)
    above = lax.ppermute(packed[2], "blk", down)
    cross = lambda pairs: [(2 * i + s, 2 * j + 1 - s) for i, j in pairs for s in (0, 1)]
    corners_below = lax.ppermute(packed[1], ("blk", "sub"), cross(up))
    corners_above = lax.ppermute(packed[3], ("blk", "sub"), cross(down))
    return below, above, beside, corners_below, corners_above


def forecast_kernel(*refs, parts, tiles, lines, ranges):
    ens, thick, wet = refs[:3]
    mem_halo, sta_halo = refs[3:8], refs[8:13]
    n_out = parts * len(ranges)
    outs = refs[13 : 13 + n_out]
    h, u, v, fu, g, m95, mf, m35, t35, inside, res = refs[13 + n_out :]
    rows, columns = thick.shape
    height, width = h.shape
    z, b, s = lax.axis_index("grid"), lax.axis_index("blk"), lax.axis_index("sub")
    lane = lax.broadcasted_iota(jnp.int32, (1, LANES), 1)
    beside_ok = jnp.where(lax.div(lane, LANES // 2) == s, 1.0, 0.0)
    below_ok = (b < tiles - 1).astype(f32)
    above_ok = (b > 0).astype(f32)
    lower = rows + PAD

    def place(ref, center, below, above, beside, corner_below, corner_above):
        ref[PAD:lower, :columns] = center
        ref[PAD:lower, columns:] = beside * beside_ok
        ref[lower : lower + HALO, :columns] = below * below_ok
        ref[PAD - HALO : PAD, :columns] = above * above_ok
        ref[lower : lower + HALO, columns:] = corner_below * beside_ok * below_ok
        ref[PAD - HALO : PAD, columns:] = corner_above * beside_ok * above_ok

    @pl.when(pl.program_id(0) == 0)
    def _():
        for ref in (h, u, v, m95, t35, inside):
            ref[:PAD] = jnp.zeros((PAD, width), f32)
            ref[lower:] = jnp.zeros((PAD, width), f32)
        place(t35, thick[...], *(ref[0, 0] for ref in sta_halo))
        place(m95, wet[...].astype(f32), *(ref[0, 1] for ref in sta_halo))
        one = lambda *shape: jnp.ones(shape, f32)
        place(inside, one(rows, columns), one(HALO, columns), one(HALO, columns), one(rows, LANES), one(HALO, LANES), one(HALO, LANES))
        for r in range(0, height, PAD):
            here = slice(r, r + PAD)
            t35[here] = DIVERGE * t35[here]
            m = m95[here]
            line = (b * rows + (r - PAD) + lax.broadcasted_iota(jnp.int32, (PAD, 1), 0)).astype(f32)
            m95[here] = (1.0 - FRICTION) * m
            m35[here] = PRESSURE * m
            mf[here] = (CORIOLIS * (2.0 * (line + 0.5) / (tiles * rows) - 1.0)) * m

    for field, ref in enumerate((h, u, v)):
        place(ref, ens[0, field], *(halo_ref[0, field] for halo_ref in mem_halo))

    def above_of(ref, r):
        return pltpu.roll(ref[:PAD], 1, 0) if r == 0 else ref[r - 1 : r - 1 + PAD]

    def below_of(ref, r):
        return pltpu.roll(ref[r : r + PAD], PAD - 1, 0) if r + PAD == height else ref[r + 1 : r + 1 + PAD]

    def across(field):
        return pltpu.roll(field, width - 1, 1) - pltpu.roll(field, 1, 1)

    def keep(field, r, value):
        size = min(PAD, lines)
        for start in range(0, PAD, size):
            domain, line = divmod(r - PAD + start, lines)
            res[field, domain, line : line + size] = value[start : start + size, :columns]

    for step in range(STEPS):
        last = step == STEPS - 1
        for r in range(0, height, PAD):
            here = slice(r, r + PAD)
            hc, uc, vc = h[here], u[here], v[here]
            a, c, d = m95[here], mf[here], m35[here]
            un = a * uc + c * vc - d * (below_of(h, r) - above_of(h, r))
            vn = a * vc - c * uc - d * across(hc)
            t = t35[here]
            fu[here] = t * un
            inner = PAD <= r < lower
            if last and inner:
                keep(1, r, un)
                keep(2, r, vn)
            if not last:
                u[here] = un
                v[here] = vn
            if inner or not last:
                g[here] = across(t * vn)
        for r in range(0, height, PAD):
            here = slice(r, r + PAD)
            if last and not PAD <= r < lower:
                continue
            hn = h[here] - ((below_of(fu, r) - above_of(fu, r)) + g[here])
            if last:
                keep(0, r, hn)
            else:
                h[here] = hn * inside[here]

    per_field = outs[0].shape[1] and lines // outs[0].shape[2]
    for shift in range(parts):
        domain = lax.rem(z + shift, parts)
        for number, (start, stop) in enumerate(ranges):
            out = outs[number * parts + shift]
            for q in range(start, stop):
                field, piece = divmod(q, per_field)
                size = out.shape[2]
                out[0, q - start] = res[field, domain, piece * size : (piece + 1) * size]


def forecast(ensemble, first, members, fields, mem_halo, sta_halo, static_at, size, ranges):
    thick, wet = fields
    rows, columns = ensemble.shape[2:]
    parts, tiles = lax.axis_size("grid"), lax.axis_size("blk")
    lines = rows // parts
    ext = pltpu.VMEM((rows + 2 * PAD, columns + LANES), f32)
    whole = pl.BlockSpec((rows, columns), lambda i: (0, 0))
    in_specs = [pl.BlockSpec((1, 3, rows, columns), lambda i: (first + i, 0, 0, 0)), whole, whole]
    in_specs += [pl.BlockSpec((1,) + x.shape[1:], lambda i: (i, 0, 0, 0)) for x in mem_halo]
    in_specs += [pl.BlockSpec((1,) + x.shape[1:], lambda i: (static_at, 0, 0, 0)) for x in sta_halo]
    shapes = [(stop - start, size, columns) for start, stop in ranges for shift in range(parts)]
    flat = pl.pallas_call(
        functools.partial(forecast_kernel, parts=parts, tiles=tiles, lines=lines, ranges=ranges),
        grid=(members,),
        in_specs=in_specs,
        out_specs=[pl.BlockSpec((1,) + s, lambda i: (i, 0, 0, 0)) for s in shapes],
        out_shape=[jax.ShapeDtypeStruct((members,) + s, f32) for s in shapes],
        scratch_shapes=[ext] * 10 + [pltpu.VMEM((3, parts, lines, columns), f32)],
        compiler_params=pltpu.CompilerParams(vmem_limit_bytes=48 << 20),
        name="forecast",
    )(ensemble, thick, wet, *mem_halo, *sta_halo)
    return [flat[i * parts : (i + 1) * parts] for i in range(len(ranges))]


def exchange(pieces):
    parts = len(pieces)
    got = [pieces[0]]
    for shift in range(1, parts):
        got.append(lax.ppermute(pieces[shift], "grid", [(i, (i + shift) % parts) for i in range(parts)]))
    return got


def rows_of(refs):
    return jnp.concatenate([ref[:, 0].reshape(-1, ref.shape[3]) for ref in refs], axis=0)


def observe_kernel(*refs, members, width):
    count, cell, value, error = refs[:4]
    pieces, (out, picked) = refs[4:-2], refs[-2:]
    q = pl.program_id(0)
    columns = width
    slots = cell.shape[1]
    cells = cell[...]
    column = lax.rem(cells, columns)
    line = lax.rem(lax.div(cells, columns), PAD)
    block = lax.div(cells, columns * PAD)
    chosen = (lax.broadcasted_iota(jnp.int32, (columns, slots), 0) == column) & (block == q)
    pick = jnp.where(chosen, 1.0, 0.0).astype(jnp.bfloat16)
    left = rows_of(pieces)
    found = 0.0
    for part in range(3):
        head = left.astype(jnp.bfloat16)
        found = found + nn(head, pick)
        left = left - head.astype(f32)
    line_of = lax.rem(lax.broadcasted_iota(jnp.int32, found.shape, 0), PAD)
    found = jnp.sum(jnp.where(line_of == line, found, 0.0).reshape(members, PAD, slots), axis=1)

    @pl.when(q == 0)
    def _():
        picked[...] = found

    @pl.when(q > 0)
    def _():
        picked[...] += found

    @pl.when(q == pl.num_programs(0) - 1)
    def _():
        p = picked[...]
        pbar = jnp.mean(p, axis=0, keepdims=True)
        valid = lax.broadcasted_iota(jnp.int32, (1, slots), 1) < count[0, 0]
        scale = jnp.where(valid, 1.0 / (error[...] * math.sqrt(members - 1)), 0.0)
        anomaly = (p - pbar) * scale
        innovation = (value[...] - pbar) * scale
        out[:members] = nt(anomaly, anomaly)
        out[members:] = nt(jnp.broadcast_to(innovation, (PAD, slots)), anomaly)


def piece_specs(pieces, offset):
    return [pl.BlockSpec((x.shape[0], 1) + x.shape[2:], lambda q, o=o: (0, q + o, 0, 0)) for x, o in zip(pieces, offset)]


def observe(pieces, count_q, members, cell, count, value, error):
    slots = cell.shape[-1]
    row = pl.BlockSpec((1, slots), lambda q: (0, 0))
    return pl.pallas_call(
        functools.partial(observe_kernel, members=members, width=pieces[0].shape[3]),
        grid=(count_q,),
        in_specs=[pl.BlockSpec(memory_space=pltpu.SMEM), row, row, row] + piece_specs(pieces, [0] * len(pieces)),
        out_specs=pl.BlockSpec((members + PAD, members), lambda q: (0, 0)),
        out_shape=jax.ShapeDtypeStruct((members + PAD, members), f32),
        scratch_shapes=[pltpu.VMEM((members, slots), f32)],
        name="observe",
    )(count.reshape(1, 1), cell.reshape(1, slots), value.reshape(1, slots), error.reshape(1, slots), *pieces)


def transform_kernel(packed, high, low, *, parts, members):
    each = members // parts
    z = lax.axis_index("grid")
    row = lax.broadcasted_iota(jnp.int32, (members, members), 0)
    col = lax.broadcasted_iota(jnp.int32, (members, members), 1)
    eye = jnp.where(row == col, 1.0, 0.0)
    system = eye + packed[:members]
    proj = nt(eye, packed[members:])[:, :1]
    wide = 2 * members
    lane = lax.broadcasted_iota(jnp.int32, (members, wide), 1)
    sub = lax.broadcasted_iota(jnp.int32, (members, wide), 0)
    tableau = jnp.concatenate([system, jnp.broadcast_to(proj, (members, members))], axis=1)

    def eliminate(p, a):
        pivot_row = jnp.sum(jnp.where(sub == p, a, 0.0), axis=0, keepdims=True)
        column = jnp.sum(jnp.where(lane == p, a, 0.0), axis=1, keepdims=True)
        pivot = jnp.sum(jnp.where(lane[:1] == p, pivot_row, 0.0), axis=1, keepdims=True)
        pivot_row = pivot_row / pivot
        return jnp.where(sub == p, pivot_row, a - column * pivot_row)

    tableau = lax.fori_loop(0, members, eliminate, tableau)
    mean_w = jnp.sum(jnp.where(lane == members, tableau, 0.0), axis=1, keepdims=True)
    total = jnp.sum(jnp.sum(system * system, axis=1, keepdims=True), axis=0, keepdims=True)
    scale = jnp.sqrt(total)

    def sweep(_, state):
        y, zz = state
        factor = 1.5 * eye - 0.5 * nn(zz, y)
        return nn(y, factor), nn(factor, zz)

    _, zz = lax.fori_loop(0, NS_STEPS, sweep, (system / scale, eye))
    weights = mean_w + zz / jnp.sqrt(scale)
    mix = weights - jnp.mean(weights, axis=0, keepdims=True) + 1.0 / members
    place, item = lax.div(col, each), lax.rem(col, each)
    true = lax.rem(z - place + parts, parts) * each + item
    mixed = nt(jnp.where(row == true, 1.0, 0.0), mix)
    tall = members * PAD
    spread = jnp.where(
        lax.div(lax.broadcasted_iota(jnp.int32, (tall, members), 0), PAD)
        == lax.broadcasted_iota(jnp.int32, (tall, members), 1),
        1.0,
        0.0,
    ).astype(jnp.bfloat16)
    same = lax.rem(lax.broadcasted_iota(jnp.int32, (tall, tall), 0), PAD) == lax.rem(
        lax.broadcasted_iota(jnp.int32, (tall, tall), 1), PAD
    )
    top = mixed.astype(jnp.bfloat16)
    rest = (mixed - top.astype(f32)).astype(jnp.bfloat16)
    for out, part in ((high, top), (low, rest)):
        tallened = nn(spread, part).astype(jnp.bfloat16)
        out[...] = jnp.where(same, nt(tallened, spread), 0.0).astype(jnp.bfloat16)


def transform(packed, members):
    parts = lax.axis_size("grid")
    tall = members * PAD
    shape = jax.ShapeDtypeStruct((tall, tall), jnp.bfloat16)
    return pl.pallas_call(
        functools.partial(transform_kernel, parts=parts, members=members),
        out_shape=[shape, shape],
        name="transform",
    )(packed)


def analysis_kernel(*refs, carried):
    high, low = refs[:2]
    pieces, out = refs[2 : -1 - carried], refs[-1]
    x = rows_of(pieces)
    top = x.astype(jnp.bfloat16)
    rest = (x - top.astype(f32)).astype(jnp.bfloat16)
    y = nn(high[...], rest) + nn(low[...], top)
    y = y + nn(high[...], top)
    out[...] = y.reshape(out.shape)


def analyse(mixers, pieces, offset, q0, q1, shape, carried):
    square = pl.BlockSpec(mixers[0].shape, lambda q: (0, 0))
    specs = [square, square] + piece_specs(pieces, offset)
    operands = [*mixers, *pieces]
    aliases = {}
    if carried is not None:
        aliases = {len(operands): 0}
        specs.append(pl.BlockSpec(memory_space=pl.ANY))
        operands.append(carried)
    return pl.pallas_call(
        functools.partial(analysis_kernel, carried=int(carried is not None)),
        grid=(q1 - q0,),
        in_specs=specs,
        out_specs=pl.BlockSpec((shape[0], 1) + shape[2:], lambda q: (0, q + q0, 0, 0)),
        out_shape=jax.ShapeDtypeStruct(shape, f32),
        input_output_aliases=aliases,
        name="analysis",
    )(*operands)


def shards(ensemble, basin_thickness, wet_indicator, obs_cell, obs_count, obs_value, obs_error):
    held, _, rows, columns = ensemble.shape
    parts = lax.axis_size("grid")
    members = held * parts
    lines = rows // parts
    size = PAD if lines % PAD == 0 else lines
    per_field = lines // size
    total = 3 * per_field
    width = size * columns // PAD
    early = max(1, held // 4)
    late = held - early
    fields = (basin_thickness, wet_indicator)
    halo_early = edges(ensemble, 0, early, fields)
    halo_late = edges(ensemble, early, late, ())
    ranges_early = [(0, per_field), (per_field, total)]
    cuts = sorted({0, per_field, 2 * per_field, total - 1, total})
    ranges_late = list(zip(cuts[:-1], cuts[1:]))
    sent_early = forecast(ensemble, 0, early, fields, halo_early, halo_early, early, size, ranges_early)
    sent_late = forecast(ensemble, early, late, fields, halo_late, halo_early, early, size, ranges_late)

    def received(pieces):
        got = exchange(pieces)
        return [x.reshape(x.shape[0], x.shape[1], PAD, width) for x in got]

    early_h = received(sent_early[0])
    late_h = received(sent_late[0])
    early_uv = received(sent_early[1])
    late_uv = [received(x) for x in sent_late[1:]]

    def woven(a, b):
        return [x for pair in zip(a, b) for x in pair]

    packed = observe(woven(early_h, late_h), per_field, members, obs_cell, obs_count, obs_value, obs_error)
    packed = lax.psum(packed, ("blk", "sub"))
    mixers = transform(packed, members)
    shape = (members, total, PAD, width)
    out = analyse(mixers, woven(early_h, late_h), [0] * (2 * parts), 0, per_field, shape, None)
    for (start, stop), pieces in zip(ranges_late[1:], late_uv):
        offset = [start - per_field, 0] * parts
        out = analyse(mixers, woven(early_uv, pieces), offset, start, stop, shape, out)
    return out.reshape(members, 3, 1, lines, columns)


def solution(mesh):
    placed = (
        P(("copy", "grid"), None, "blk", "sub"),
        P(("copy", "blk"), "sub"),
        P(("copy", "blk"), "sub"),
        P(("copy", "blk"), "grid", "sub"),
        P(("copy", "blk"), "grid", "sub"),
        P(("copy", "blk"), "grid", "sub"),
        P(("copy", "blk"), "grid", "sub"),
    )
    return jax.shard_map(
        shards,
        mesh=mesh,
        in_specs=placed,
        out_specs=P("copy", None, "blk", "grid", "sub"),
        check_vma=False,
    )
```

time: 588 us -> 349 us (0.59)
  waiting for transfers between devices: 280 us -> 77.6 us
  local copies, waits for them, and re-layouts: 112 us -> 4.88 us
  Pallas kernels: 0 us -> 106 us
  other arithmetic: 104 us -> 0 us
  starting transfers between devices: 49.3 us -> 147 us
  matrix products: 22.2 us -> 0 us
    all_to_all x1 -> x0, waiting for transfers between devices: 273 us -> none  [shards(): lax.all_to_all(dynamic_vector, 'grid', split_axis=2, concat_axis=0, tiled...]
    pallas_call x0 -> x10, Pallas kernels: none -> 106 us  [the longest x2 50.5 us: forecast(): pl.pallas_call(functools.partial(forecast_kernel, parts=parts, tiles=tile...]
    ppermute x16 -> x24, starting transfers between devices: 42.7 us -> 147 us  [the longest x18 141 us: exchange(): lax.ppermute(pieces[shift], 'grid', [(i, (i + shift) % parts) for i in ra...]
    ppermute x16 -> x24, waiting for transfers between devices: 6.93 us -> 77.6 us  [the longest x18 67.4 us: exchange(): lax.ppermute(pieces[shift], 'grid', [(i, (i + shift) % parts) for i in ra...]
    another operation x11 -> x0, other arithmetic: 61.2 us -> none  [the longest x4 40 us: thin_step(): jnp.stack([inner_depth * first_new, inner_depth * second_new], axis=1)]
    slice x14 -> x0, local copies, waits for them, and re-layouts: 26.9 us -> none  [the longest x1 10.2 us: thin_step(): dynamic_vector[:, 2]]
    sub x2 -> x0, other arithmetic: 24.1 us -> none  [thin_step(): height_new = height - DIVERGE * divergence]
    unnamed x30 -> x48, local copies, waits for them, and re-layouts: 27.9 us -> 4.88 us
  transfers between devices with their start and end apart: 17 -> 24, of which waited for: 7 -> 5; matrix products, arithmetic and copies ran while one was open for 2% -> 0% of each run, Pallas kernels for 0% -> 27%
where the time goes in v1:
time: 349 us; the launch traced here: 348 us
  starting transfers between devices  147 us (42%)
  Pallas kernels  106 us (30%)
  waiting for transfers between devices  77.6 us (22%)
  blocking collectives  11.8 us (3%)
  local copies, waits for them, and re-layouts  4.88 us (1%)
    ppermute x18, starting transfers between devices, exchange(): lax.ppermute(pieces[shift], 'grid', [(i, (i + shift) % parts) for i in ra...  141 us
    ppermute x18, waiting for transfers between devices, exchange(): lax.ppermute(pieces[shift], 'grid', [(i, (i + shift) % parts) for i in ra...  67.4 us
    pallas_call x2, Pallas kernels, forecast(): pl.pallas_call(functools.partial(forecast_kernel, parts=parts, tiles=tile...  50.5 us
    pallas_call x4, Pallas kernels, analyse(): pl.pallas_call(functools.partial(analysis_kernel, carried=int(carried is...  24.9 us
    pallas_call x2, Pallas kernels, edges(): pl.pallas_call(functools.partial(pack_kernel, members=members, two=two, s...  12.8 us
    pallas_call x1, Pallas kernels, transform(): pl.pallas_call(functools.partial(transform_kernel, parts=parts, members=m...  12.2 us
    psum x1, blocking collectives, shards(): packed = lax.psum(packed, ('blk', 'sub'))  11.8 us
    ppermute x2, waiting for transfers between devices, halo(): lax.ppermute(packed[1], ('blk', 'sub'), [(0, 3), (3, 0), (1, 2), (2, 1)])  10.1 us
  transfers between devices with their start and end apart: 24, of which 5 were waited for; matrix products, arithmetic and copies ran while one was open for 0% of the time, Pallas kernels for 27%

profile of v1, /device:TPU:0, one launch (start us, length us, event | category | flops | bytes accessed | tf_op | source)
XLA Modules:
  0.0 348.2 jit_solution(4607390813983349600)
XLA Ops:
  0.0 8.5 %edges.3 = (f32[12,3,4,512]{3,2,1,0:T(4,128)}, f32[12,3,4,128]{3,2,1,0:T(4,128)}, f32[12,3,128,128]{3,2,1,0:T(8,128)}) custom-call(f32[16,3,128,512]{3,2,1,0:T(8,128)} %refs_0_.7, f32[16,3,128,512]{3,2,1,0:T(8,128)} %refs_0_.7, f32[16,3,128,512]{3,2,1,0:T(8,128)} %refs_0_.7, f32[16,3,128,512]{3,2,1,0:T(8,128)} %refs_0_.7, f32[16,3,128,512]{3,2,1,0:T(8,128)} %refs_0_.7, ...), custom_call_target="tpu_custom_call" | custom-call | tf_op jit(solution)/shard_map/edges/pallas_call | solution.py:126
  8.5 0.0 copy-start.3
  8.6 0.0 copy-start.4
  8.6 0.5 collective-permute-start.4
  9.1 4.2 %edges.2 = (f32[5,3,4,512]{3,2,1,0:T(4,128)}, f32[5,3,4,128]{3,2,1,0:T(4,128)}, f32[5,3,128,128]{3,2,1,0:T(8,128)}) custom-call(f32[16,3,128,512]{3,2,1,0:T(8,128)} %refs_0_.7, f32[16,3,128,512]{3,2,1,0:T(8,128)} %refs_0_.7, f32[16,3,128,512]{3,2,1,0:T(8,128)} %refs_0_.7, f32[16,3,128,512]{3,2,1,0:T(8,128)} %refs_0_.7, f32[16,3,128,512]{3,2,1,0:T(8,128)} %refs_0_.7, ...), custom_call_target="tpu_custom_call" | custom-call | tf_op jit(solution)/shard_map/edges/pallas_call | solution.py:126
  13.3 0.2 collective-permute-start.1
  13.5 2.9 collective-permute-start
  16.4 0.0 collective-permute-start.3
  16.4 1.2 collective-permute-start.2
  17.6 9.1 %collective-permute-done.2.refs_6_.refs_7_.refs_11_.refs_12_ = f32[5,3,4,128]{3,2,1,0:T(4,128)S(1)} collective-permute-done((f32[5,3,4,128]{3,2,1,0:T(4,128)}, f32[5,3,4,128]{3,2,1,0:T(4,128)S(1)}, u32[]{:S(2)}, u32[]{:S(2)}) %collective-permute-start.2) | collective-permute-done | bytes 30752 | tf_op jit(solution)/shard_map/ppermute | solution.py:142
  26.7 0.0 collective-permute-done.refs_3_.refs_4_.refs_8_.refs_9_
  26.7 0.0 collective-permute-done.1.refs_5_.refs_10_
  26.7 13.3 %forecast.2 = (f32[4,4,8,512]{3,2,1,0:T(8,128)S(1)}, f32[4,4,8,512]{3,2,1,0:T(8,128)S(1)}, f32[4,4,8,512]{3,2,1,0:T(8,128)S(1)}, f32[4,4,8,512]{3,2,1,0:T(8,128)...) custom-call(f32[16,3,128,512]{3,2,1,0:T(8,128)} %refs_0_.7, ...), custom_call_target="tpu_custom_call" | custom-call | tf_op jit(solution)/shard_map/forecast/pallas_call | solution.py:264
  40.0 0.8 copy-done.1
  40.8 1.5 collective-permute-start.6
  42.3 1.5 collective-permute-start.5
  43.8 1.6 collective-permute-start.12
  45.4 1.1 collective-permute-done.5.refs_6_.refs_7_
  46.4 2.6 collective-permute-start.14
  49.1 0.0 collective-permute-done.3.refs_3_.refs_4_
  49.1 0.3 collective-permute-start.8
  49.4 0.0 collective-permute-done.4.refs_5_
  49.4 2.2 collective-permute-start.10
  51.5 37.2 %forecast.3 = (f32[12,4,8,512]{3,2,1,0:T(8,128)S(1)}, f32[12,4,8,512]{3,2,1,0:T(8,128)S(1)}, f32[12,4,8,512]{3,2,1,0:T(8,128)}, f32[12,4,8,512]{3,2,1,0:T(8,128)...) custom-call(f32[16,3,128,512]{3,2,1,0:T(8,128)} %refs_0_.7, ...), custom_call_target="tpu_custom_call" | custom-call | tf_op jit(solution)/shard_map/forecast/pallas_call | solution.py:264
  88.7 0.9 copy-done.2
  89.6 0.9 copy-done.6
  90.5 0.7 copy-done.7
  91.2 0.0 collective-permute-done.6.refs_6_.refs_4_
  91.2 0.0 collective-permute-start.7
  91.2 22.2 %collective-permute-done.8.refs_8_.refs_6_ = f32[4,4,8,512]{3,2,1,0:T(8,128)S(1)} collective-permute-done((f32[4,4,8,512]{3,2,1,0:T(8,128)S(1)}, f32[4,4,8,512]{3,2,1,0:T(8,128)S(1)}, u32[]{:S(2)}, u32[]{:S(2)}) %collective-permute-start.8) | collective-permute-done | bytes 262176 | tf_op jit(solution)/shard_map/ppermute | solution.py:281
  113.4 0.0 collective-permute-start.18
  113.4 0.0 collective-permute-done.10.refs_10_.refs_8_
  113.4 3.8 %collective-permute-start.16 = (f32[4,8,8,512]{3,2,1,0:T(8,128)S(1)}, f32[4,8,8,512]{3,2,1,0:T(8,128)S(1)}, u32[]{:S(2)}, u32[]{:S(2)}) collective-permute-start(f32[4,8,8,512]{3,2,1,0:T(8,128)S(1)} %get-tuple-element.59), channel_id=1, source_target_pairs={{0,12},{4,0},{8,4},{12,8},{1,13},{5,1},{9,5},{13,9},{2,14},{6,2},{... | collective-permute-start | bytes 1572872 | tf_op jit(solution)/shard_map/ppermute | solution.py:281
  117.2 0.0 collective-permute-done.12.refs_4_
  117.2 16.5 %collective-permute-start.9 = (f32[12,4,8,512]{3,2,1,0:T(8,128)}, f32[12,4,8,512]{3,2,1,0:T(8,128)S(1)}, u32[]{:S(2)}, u32[]{:S(2)}) collective-permute-start(f32[12,4,8,512]{3,2,1,0:T(8,128)} %get-tuple-element.48), channel_id=1, source_target_pairs={{0,8},{4,12},{8,0},{12,4},{1,9},{5,13},{9,1},{13,5},{2,10},{6,14},... | collective-permute-start | bytes 2359304 | tf_op jit(solution)/shard_map/ppermute | solution.py:281
  133.7 0.0 collective-permute-done.14.refs_6_
  133.7 0.9 collective-permute-start.11
  134.6 10.2 %collective-permute-done.16.refs_8_ = f32[4,8,8,512]{3,2,1,0:T(8,128)S(1)} collective-permute-done((f32[4,8,8,512]{3,2,1,0:T(8,128)S(1)}, f32[4,8,8,512]{3,2,1,0:T(8,128)S(1)}, u32[]{:S(2)}, u32[]{:S(2)}) %collective-permute-start.16) | collective-permute-done | bytes 524320 | tf_op jit(solution)/shard_map/ppermute | solution.py:281
  144.9 18.9 %collective-permute-start.21 = (f32[12,4,8,512]{3,2,1,0:T(8,128)}, f32[12,4,8,512]{3,2,1,0:T(8,128)S(1)}, u32[]{:S(2)}, u32[]{:S(2)}) collective-permute-start(f32[12,4,8,512]{3,2,1,0:T(8,128)} %get-tuple-element.66), channel_id=1, source_target_pairs={{0,4},{4,8},{8,12},{12,0},{1,5},{5,9},{9,13},{13,1},{2,6},{6,10},{... | collective-permute-start | bytes 2359304 | tf_op jit(solution)/shard_map/ppermute | solution.py:281
  163.8 0.0 collective-permute-done.18.refs_5_
  163.8 0.9 copy-done.20
  164.7 13.7 %collective-permute-start.22 = (f32[12,4,8,512]{3,2,1,0:T(8,128)}, f32[12,4,8,512]{3,2,1,0:T(8,128)S(1)}, u32[]{:S(2)}, u32[]{:S(2)}) collective-permute-start(f32[12,4,8,512]{3,2,1,0:T(8,128)} %get-tuple-element.67), channel_id=1, source_target_pairs={{0,8},{4,12},{8,0},{12,4},{1,9},{5,13},{9,1},{13,5},{2,10},{6,14},... | collective-permute-start | bytes 2359304 | tf_op jit(solution)/shard_map/ppermute | solution.py:281
  178.4 0.0 collective-permute-done.7.refs_7_.refs_5_
  178.4 0.4 collective-permute-start.23
  178.9 35.0 %collective-permute-done.9.refs_9_.refs_7_ = f32[12,4,8,512]{3,2,1,0:T(8,128)S(1)} collective-permute-done((f32[12,4,8,512]{3,2,1,0:T(8,128)}, f32[12,4,8,512]{3,2,1,0:T(8,128)S(1)}, u32[]{:S(2)}, u32[]{:S(2)}) %collective-permute-start.9) | collective-permute-done | bytes 786464 | tf_op jit(solution)/shard_map/ppermute | solution.py:281
  213.8 0.0 collective-permute-start.19
  213.9 27.9 %collective-permute-start.20 = (f32[12,3,8,512]{3,2,1,0:T(8,128)S(1)}, f32[12,3,8,512]{3,2,1,0:T(8,128)}, u32[]{:S(2)}, u32[]{:S(2)}) collective-permute-start(f32[12,3,8,512]{3,2,1,0:T(8,128)S(1)} %get-tuple-element.64), channel_id=1, source_target_pairs={{0,12},{4,0},{8,4},{12,8},{1,13},{5,1},{9,5},{13,9},{2,14},{6,2},{... | collective-permute-start | bytes 1769480 | tf_op jit(solution)/shard_map/ppermute | solution.py:281
  241.8 0.0 collective-permute-done.21.refs_5_
  241.8 26.7 %collective-permute-start.13 = (f32[12,1,8,512]{3,2,1,0:T(8,128)S(1)}, f32[12,1,8,512]{3,2,1,0:T(8,128)S(1)}, u32[]{:S(2)}, u32[]{:S(2)}) collective-permute-start(f32[12,1,8,512]{3,2,1,0:T(8,128)S(1)} %get-tuple-element.56), channel_id=1, source_target_pairs={{0,4},{4,8},{8,12},{12,0},{1,5},{5,9},{9,13},{13,1},{2,6},{6,10},{... | collective-permute-start | bytes 589832 | tf_op jit(solution)/shard_map/ppermute | solution.py:281
  268.5 0.0 collective-permute-done.22.refs_7_
  268.5 1.9 collective-permute-start.15
  270.4 22.0 %collective-permute-start.17 = (f32[12,1,8,512]{3,2,1,0:T(8,128)S(1)}, f32[12,1,8,512]{3,2,1,0:T(8,128)}, u32[]{:S(2)}, u32[]{:S(2)}) collective-permute-start(f32[12,1,8,512]{3,2,1,0:T(8,128)S(1)} %get-tuple-element.60), channel_id=1, source_target_pairs={{0,12},{4,0},{8,4},{12,8},{1,13},{5,1},{9,5},{13,9},{2,14},{6,2},{... | collective-permute-start | bytes 589832 | tf_op jit(solution)/shard_map/ppermute | solution.py:281
  293.1 5.4 %observe.1 = f32[72,64]{1,0:T(8,128)} custom-call(s32[1,1]{1,0:T(1,128)} %bitcast.7.refs_0_, s32[1,64]{1,0:T(1,128)} %bitcast.8, f32[1,64]{1,0:T(1,128)} %bitcast.9, f32[1,64]{1,0:T(1,128)} %bitcast.10, f32[4,4,8,512]{3,2,1,0:T(8,128)} %copy-done.5, f32[12,4,8,512]{3,2,1,0:T(8,128)} %copy-done.2, f32[4,4,8,512]{3,2,1,0:T(8,128)} %copy-done.14, ...), custom_call_target="tpu_custom_call" | custom-call | tf_op jit(solution)/shard_map/observe/pallas_call | solution.py:337
  298.5 11.8 %psum.7.packed = f32[72,64]{1,0:T(8,128)} all-reduce(f32[72,64]{1,0:T(8,128)} %observe.1), channel_id=1, replica_groups=mesh['copy'=2,'grid'=4,'blk'=2,'sub'=2] {'blk','sub'}, use_global_device_ids=true, to_apply=%region_0.0 | all-reduce | flops 4608 | bytes 36864 | tf_op jit(solution)/shard_map/psum | solution.py:476
  310.4 12.2 %transform.1 = (bf16[512,512]{1,0:T(8,128)(2,1)}, bf16[512,512]{1,0:T(8,128)(2,1)}) custom-call(f32[72,64]{1,0:T(8,128)} %psum.7.packed), custom_call_target="tpu_custom_call" | custom-call | tf_op jit(solution)/shard_map/transform/pallas_call | solution.py:405
  322.6 7.5 %analysis.4.refs_10_ = f32[64,12,8,512]{3,2,1,0:T(8,128)} custom-call(bf16[512,512]{1,0:T(8,128)(2,1)} %get-tuple-element.51.refs_0_, bf16[512,512]{1,0:T(8,128)(2,1)} %get-tuple-element.52.refs_1_, f32[4,4,8,512]{3,2,1,0:T(8,128)} %copy-done.5, f32[12,4,8,512]{3,2,1,0:T(8,128)} %copy-done.2, f32[4,4,8,512]{3,2,1,0:T(8,128)} %copy-done.14, ...), custom_call_target="tpu_custom_call" | custom-call | tf_op jit(solution)/shard_map/analysis/pallas_call | solution.py:432
  330.1 7.5 %analysis.5.refs_10_ = f32[64,12,8,512]{3,2,1,0:T(8,128)} custom-call(bf16[512,512]{1,0:T(8,128)(2,1)} %get-tuple-element.51.refs_0_, bf16[512,512]{1,0:T(8,128)(2,1)} %get-tuple-element.52.refs_1_, f32[4,8,8,512]{3,2,1,0:T(8,128)} %copy-done.1, f32[12,4,8,512]{3,2,1,0:T(8,128)} %get-tuple-element.65.refs_3_, ...), custom_call_target="tpu_custom_call", output_to_operand_aliasing={{}: (10, {})} | custom-call | tf_op jit(solution)/shard_map/analysis/pallas_call | solution.py:432
  337.6 0.0 collective-permute-done.20.refs_9_
  337.6 6.5 %analysis.6.refs_10_ = f32[64,12,8,512]{3,2,1,0:T(8,128)} custom-call(bf16[512,512]{1,0:T(8,128)(2,1)} %get-tuple-element.51.refs_0_, bf16[512,512]{1,0:T(8,128)(2,1)} %get-tuple-element.52.refs_1_, f32[4,8,8,512]{3,2,1,0:T(8,128)} %copy-done.1, f32[12,3,8,512]{3,2,1,0:T(8,128)} %copy-done.6, ...), custom_call_target="tpu_custom_call", output_to_operand_aliasing={{}: (10, {})} | custom-call | tf_op jit(solution)/shard_map/analysis/pallas_call | solution.py:432
  344.1 0.0 collective-permute-done.13.refs_5_
  344.1 0.0 collective-permute-done.15.refs_7_
  344.1 0.0 collective-permute-done.17.refs_9_
  344.1 0.7 copy-done.21
  344.8 3.4 analysis.7
  (43 shorter events, 0.1 us)
Async XLA Ops:
  8.5 7.9 %copy-start.22 = (f32[12,3,4,512]{3,2,1,0:T(4,128)S(1)}, f32[12,3,4,512]{3,2,1,0:T(4,128)}, u32[]{:S(2)}) copy-start(f32[12,3,4,512]{3,2,1,0:T(4,128)} %get-tuple-element.41) | copy-start | bytes 884740
  8.5 18.1 %copy-start.3 = (f32[128,512]{1,0:T(8,128)S(1)}, f32[128,512]{1,0:T(8,128)}, u32[]{:S(2)}) copy-start(f32[128,512]{1,0:T(8,128)} %refs_1_.7) | copy-start | bytes 786436
  8.6 18.1 %copy-start.4 = (s32[128,512]{1,0:T(8,128)S(1)}, s32[128,512]{1,0:T(8,128)}, u32[]{:S(2)}) copy-start(s32[128,512]{1,0:T(8,128)} %refs_2_.7) | copy-start | bytes 786436
  8.6 40.8 %collective-permute-start.4 = (f32[12,3,128,128]{3,2,1,0:T(8,128)}, f32[12,3,128,128]{3,2,1,0:T(8,128)}, u32[]{:S(2)}, u32[]{:S(2)}) collective-permute-start(f32[12,3,128,128]{3,2,1,0:T(8,128)} %get-tuple-element.42), channel_id=1, source_target_pairs={{0,1},{1,0},{2,3},{3,2},{4,5},{5,4},{6,7},{7,6},{8,9},{9,8},{10,11... | collective-permute-start | bytes 7077896 | tf_op jit(solution)/shard_map/ppermute | solution.py:139
  13.3 29.0 %copy-start.23 = (f32[12,3,4,128]{3,2,1,0:T(4,128)S(1)}, f32[12,3,4,128]{3,2,1,0:T(4,128)}, u32[]{:S(2)}) copy-start(f32[12,3,4,128]{3,2,1,0:T(4,128)} %get-tuple-element.43) | copy-start | bytes 221188
  13.3 13.3 %collective-permute-start.1 = (f32[5,3,128,128]{3,2,1,0:T(8,128)}, f32[5,3,128,128]{3,2,1,0:T(8,128)S(1)}, u32[]{:S(2)}, u32[]{:S(2)}) collective-permute-start(f32[5,3,128,128]{3,2,1,0:T(8,128)} %get-tuple-element.38), channel_id=1, source_target_pairs={{0,1},{1,0},{2,3},{3,2},{4,5},{5,4},{6,7},{7,6},{8,9},{9,8},{10,11... | collective-permute-start | bytes 2949128 | tf_op jit(solution)/shard_map/ppermute | solution.py:139
  13.5 13.2 %collective-permute-start = (f32[5,3,4,512]{3,2,1,0:T(4,128)}, f32[5,3,4,512]{3,2,1,0:T(4,128)S(1)}, u32[]{:S(2)}, u32[]{:S(2)}) collective-permute-start(f32[5,3,4,512]{3,2,1,0:T(4,128)} %get-tuple-element.37), channel_id=1, source_target_pairs={{0,2},{2,0},{1,3},{3,1},{4,6},{6,4},{5,7},{7,5},{8,10},{10,8},{9,1... | collective-permute-start | bytes 368648 | tf_op jit(solution)/shard_map/ppermute | solution.py:141
  16.4 32.7 %collective-permute-start.3 = (f32[12,3,4,512]{3,2,1,0:T(4,128)S(1)}, f32[12,3,4,512]{3,2,1,0:T(4,128)S(1)}, u32[]{:S(2)}, u32[]{:S(2)}) collective-permute-start(f32[12,3,4,512]{3,2,1,0:T(4,128)S(1)} %copy-done.22), channel_id=1, source_target_pairs={{0,2},{2,0},{1,3},{3,1},{4,6},{6,4},{5,7},{7,5},{8,10},{10,8},{9,1... | collective-permute-start | bytes 884744 | tf_op jit(solution)/shard_map/ppermute | solution.py:141
  16.4 10.2 %collective-permute-start.2 = (f32[5,3,4,128]{3,2,1,0:T(4,128)}, f32[5,3,4,128]{3,2,1,0:T(4,128)S(1)}, u32[]{:S(2)}, u32[]{:S(2)}) collective-permute-start(f32[5,3,4,128]{3,2,1,0:T(4,128)} %get-tuple-element.39), channel_id=1, source_target_pairs={{0,3},{3,0},{1,2},{2,1},{4,7},{7,4},{5,6},{6,5},{8,11},{11,8},{9,1... | collective-permute-start | bytes 92168 | tf_op jit(solution)/shard_map/ppermute | solution.py:142
  26.7 24.8 %copy-start = (f32[5,3,128,128]{3,2,1,0:T(8,128)}, f32[5,3,128,128]{3,2,1,0:T(8,128)S(1)}, u32[]{:S(2)}) copy-start(f32[5,3,128,128]{3,2,1,0:T(8,128)S(1)} %collective-permute-done.1.refs_5_.refs_10_) | copy-start | bytes 2949124
  40.0 0.8 copy-start.1
  40.8 47.9 %copy-start.5 = (f32[4,4,8,512]{3,2,1,0:T(8,128)}, f32[4,4,8,512]{3,2,1,0:T(8,128)S(1)}, u32[]{:S(2)}) copy-start(f32[4,4,8,512]{3,2,1,0:T(8,128)S(1)} %get-tuple-element.40.refs_4_.refs_2_) | copy-start | bytes 786436
  40.8 50.4 %collective-permute-start.6 = (f32[4,4,8,512]{3,2,1,0:T(8,128)S(1)}, f32[4,4,8,512]{3,2,1,0:T(8,128)S(1)}, u32[]{:S(2)}, u32[]{:S(2)}) collective-permute-start(f32[4,4,8,512]{3,2,1,0:T(8,128)S(1)} %get-tuple-element.45), channel_id=1, source_target_pairs={{0,4},{4,8},{8,12},{12,0},{1,5},{5,9},{9,13},{13,1},{2,6},{6,10},{... | collective-permute-start | bytes 786440 | tf_op jit(solution)/shard_map/ppermute | solution.py:281
  42.3 4.1 %collective-permute-start.5 = (f32[12,3,4,128]{3,2,1,0:T(4,128)S(1)}, f32[12,3,4,128]{3,2,1,0:T(4,128)S(1)}, u32[]{:S(2)}, u32[]{:S(2)}) collective-permute-start(f32[12,3,4,128]{3,2,1,0:T(4,128)S(1)} %copy-done.23), channel_id=1, source_target_pairs={{0,3},{3,0},{1,2},{2,1},{4,7},{7,4},{5,6},{6,5},{8,11},{11,8},{9,1... | collective-permute-start | bytes 221192 | tf_op jit(solution)/shard_map/ppermute | solution.py:142
  43.8 73.4 %collective-permute-start.12 = (f32[4,8,8,512]{3,2,1,0:T(8,128)S(1)}, f32[4,8,8,512]{3,2,1,0:T(8,128)S(1)}, u32[]{:S(2)}, u32[]{:S(2)}) collective-permute-start(f32[4,8,8,512]{3,2,1,0:T(8,128)S(1)} %get-tuple-element.55), channel_id=1, source_target_pairs={{0,4},{4,8},{8,12},{12,0},{1,5},{5,9},{9,13},{13,1},{2,6},{6,10},{... | collective-permute-start | bytes 1572872 | tf_op jit(solution)/shard_map/ppermute | solution.py:281
  46.4 87.3 %collective-permute-start.14 = (f32[4,8,8,512]{3,2,1,0:T(8,128)S(1)}, f32[4,8,8,512]{3,2,1,0:T(8,128)S(1)}, u32[]{:S(2)}, u32[]{:S(2)}) collective-permute-start(f32[4,8,8,512]{3,2,1,0:T(8,128)S(1)} %get-tuple-element.57), channel_id=1, source_target_pairs={{0,8},{4,12},{8,0},{12,4},{1,9},{5,13},{9,1},{13,5},{2,10},{6,14},... | collective-permute-start | bytes 1572872 | tf_op jit(solution)/shard_map/ppermute | solution.py:281
  49.1 64.3 %collective-permute-start.8 = (f32[4,4,8,512]{3,2,1,0:T(8,128)S(1)}, f32[4,4,8,512]{3,2,1,0:T(8,128)S(1)}, u32[]{:S(2)}, u32[]{:S(2)}) collective-permute-start(f32[4,4,8,512]{3,2,1,0:T(8,128)S(1)} %get-tuple-element.47), channel_id=1, source_target_pairs={{0,8},{4,12},{8,0},{12,4},{1,9},{5,13},{9,1},{13,5},{2,10},{6,14},... | collective-permute-start | bytes 786440 | tf_op jit(solution)/shard_map/ppermute | solution.py:281
  49.4 64.0 %collective-permute-start.10 = (f32[4,4,8,512]{3,2,1,0:T(8,128)S(1)}, f32[4,4,8,512]{3,2,1,0:T(8,128)S(1)}, u32[]{:S(2)}, u32[]{:S(2)}) collective-permute-start(f32[4,4,8,512]{3,2,1,0:T(8,128)S(1)} %get-tuple-element.49), channel_id=1, source_target_pairs={{0,12},{4,0},{8,4},{12,8},{1,13},{5,1},{9,5},{13,9},{2,14},{6,2},{... | collective-permute-start | bytes 786440 | tf_op jit(solution)/shard_map/ppermute | solution.py:281
  88.7 0.9 copy-start.2
  89.6 0.9 copy-start.6
  90.5 0.7 copy-start.7
  91.2 26.0 %copy-start.14 = (f32[4,4,8,512]{3,2,1,0:T(8,128)}, f32[4,4,8,512]{3,2,1,0:T(8,128)S(1)}, u32[]{:S(2)}) copy-start(f32[4,4,8,512]{3,2,1,0:T(8,128)S(1)} %collective-permute-done.6.refs_6_.refs_4_) | copy-start | bytes 786436
  91.2 87.3 %collective-permute-start.7 = (f32[12,4,8,512]{3,2,1,0:T(8,128)S(1)}, f32[12,4,8,512]{3,2,1,0:T(8,128)S(1)}, u32[]{:S(2)}, u32[]{:S(2)}) collective-permute-start(f32[12,4,8,512]{3,2,1,0:T(8,128)S(1)} %get-tuple-element.46), channel_id=1, source_target_pairs={{0,4},{4,8},{8,12},{12,0},{1,5},{5,9},{9,13},{13,1},{2,6},{6,10},{... | collective-permute-start | bytes 2359304 | tf_op jit(solution)/shard_map/ppermute | solution.py:281
  113.4 3.8 %copy-start.15 = (f32[4,4,8,512]{3,2,1,0:T(8,128)}, f32[4,4,8,512]{3,2,1,0:T(8,128)S(1)}, u32[]{:S(2)}) copy-start(f32[4,4,8,512]{3,2,1,0:T(8,128)S(1)} %collective-permute-done.8.refs_8_.refs_6_) | copy-start | bytes 786436
  113.4 50.4 %collective-permute-start.18 = (f32[12,3,8,512]{3,2,1,0:T(8,128)S(1)}, f32[12,3,8,512]{3,2,1,0:T(8,128)S(1)}, u32[]{:S(2)}, u32[]{:S(2)}) collective-permute-start(f32[12,3,8,512]{3,2,1,0:T(8,128)S(1)} %get-tuple-element.62), channel_id=1, source_target_pairs={{0,4},{4,8},{8,12},{12,0},{1,5},{5,9},{9,13},{13,1},{2,6},{6,10},{... | collective-permute-start | bytes 1769480 | tf_op jit(solution)/shard_map/ppermute | solution.py:281
  113.4 179.7 %copy-start.16 = (f32[4,4,8,512]{3,2,1,0:T(8,128)}, f32[4,4,8,512]{3,2,1,0:T(8,128)S(1)}, u32[]{:S(2)}) copy-start(f32[4,4,8,512]{3,2,1,0:T(8,128)S(1)} %collective-permute-done.10.refs_10_.refs_8_) | copy-start | bytes 786436
  113.4 31.5 %collective-permute-start.16 = (f32[4,8,8,512]{3,2,1,0:T(8,128)S(1)}, f32[4,8,8,512]{3,2,1,0:T(8,128)S(1)}, u32[]{:S(2)}, u32[]{:S(2)}) collective-permute-start(f32[4,8,8,512]{3,2,1,0:T(8,128)S(1)} %get-tuple-element.59), channel_id=1, source_target_pairs={{0,12},{4,0},{8,4},{12,8},{1,13},{5,1},{9,5},{13,9},{2,14},{6,2},{... | collective-permute-start | bytes 1572872 | tf_op jit(solution)/shard_map/ppermute | solution.py:281
  117.2 212.8 %copy-start.8 = (f32[4,8,8,512]{3,2,1,0:T(8,128)}, f32[4,8,8,512]{3,2,1,0:T(8,128)S(1)}, u32[]{:S(2)}) copy-start(f32[4,8,8,512]{3,2,1,0:T(8,128)S(1)} %collective-permute-done.12.refs_4_) | copy-start | bytes 1572868
  117.2 96.6 %collective-permute-start.9 = (f32[12,4,8,512]{3,2,1,0:T(8,128)}, f32[12,4,8,512]{3,2,1,0:T(8,128)S(1)}, u32[]{:S(2)}, u32[]{:S(2)}) collective-permute-start(f32[12,4,8,512]{3,2,1,0:T(8,128)} %get-tuple-element.48), channel_id=1, source_target_pairs={{0,8},{4,12},{8,0},{12,4},{1,9},{5,13},{9,1},{13,5},{2,10},{6,14},... | collective-permute-start | bytes 2359304 | tf_op jit(solution)/shard_map/ppermute | solution.py:281
  133.7 196.3 %copy-start.9 = (f32[4,8,8,512]{3,2,1,0:T(8,128)}, f32[4,8,8,512]{3,2,1,0:T(8,128)S(1)}, u32[]{:S(2)}) copy-start(f32[4,8,8,512]{3,2,1,0:T(8,128)S(1)} %collective-permute-done.14.refs_6_) | copy-start | bytes 1572868
  133.7 80.1 %collective-permute-start.11 = (f32[12,4,8,512]{3,2,1,0:T(8,128)}, f32[12,4,8,512]{3,2,1,0:T(8,128)S(1)}, u32[]{:S(2)}, u32[]{:S(2)}) collective-permute-start(f32[12,4,8,512]{3,2,1,0:T(8,128)} %get-tuple-element.50), channel_id=1, source_target_pairs={{0,12},{4,0},{8,4},{12,8},{1,13},{5,1},{9,5},{13,9},{2,14},{6,2},{... | collective-permute-start | bytes 2359304 | tf_op jit(solution)/shard_map/ppermute | solution.py:281
  144.9 185.2 %copy-start.10 = (f32[4,8,8,512]{3,2,1,0:T(8,128)}, f32[4,8,8,512]{3,2,1,0:T(8,128)S(1)}, u32[]{:S(2)}) copy-start(f32[4,8,8,512]{3,2,1,0:T(8,128)S(1)} %collective-permute-done.16.refs_8_) | copy-start | bytes 1572868
  144.9 96.9 %collective-permute-start.21 = (f32[12,4,8,512]{3,2,1,0:T(8,128)}, f32[12,4,8,512]{3,2,1,0:T(8,128)S(1)}, u32[]{:S(2)}, u32[]{:S(2)}) collective-permute-start(f32[12,4,8,512]{3,2,1,0:T(8,128)} %get-tuple-element.66), channel_id=1, source_target_pairs={{0,4},{4,8},{8,12},{12,0},{1,5},{5,9},{9,13},{13,1},{2,6},{6,10},{... | collective-permute-start | bytes 2359304 | tf_op jit(solution)/shard_map/ppermute | solution.py:281
  163.8 0.9 copy-start.20
  164.7 103.8 %collective-permute-start.22 = (f32[12,4,8,512]{3,2,1,0:T(8,128)}, f32[12,4,8,512]{3,2,1,0:T(8,128)S(1)}, u32[]{:S(2)}, u32[]{:S(2)}) collective-permute-start(f32[12,4,8,512]{3,2,1,0:T(8,128)} %get-tuple-element.67), channel_id=1, source_target_pairs={{0,8},{4,12},{8,0},{12,4},{1,9},{5,13},{9,1},{13,5},{2,10},{6,14},... | collective-permute-start | bytes 2359304 | tf_op jit(solution)/shard_map/ppermute | solution.py:281
  178.4 113.9 %copy-start.11 = (f32[12,4,8,512]{3,2,1,0:T(8,128)}, f32[12,4,8,512]{3,2,1,0:T(8,128)S(1)}, u32[]{:S(2)}) copy-start(f32[12,4,8,512]{3,2,1,0:T(8,128)S(1)} %collective-permute-done.7.refs_7_.refs_5_) | copy-start | bytes 2359300
  178.4 91.9 %collective-permute-start.23 = (f32[12,4,8,512]{3,2,1,0:T(8,128)}, f32[12,4,8,512]{3,2,1,0:T(8,128)S(1)}, u32[]{:S(2)}, u32[]{:S(2)}) collective-permute-start(f32[12,4,8,512]{3,2,1,0:T(8,128)} %get-tuple-element.68), channel_id=1, source_target_pairs={{0,12},{4,0},{8,4},{12,8},{1,13},{5,1},{9,5},{13,9},{2,14},{6,2},{... | collective-permute-start | bytes 2359304 | tf_op jit(solution)/shard_map/ppermute | solution.py:281
  213.8 79.2 %copy-start.12 = (f32[12,4,8,512]{3,2,1,0:T(8,128)}, f32[12,4,8,512]{3,2,1,0:T(8,128)S(1)}, u32[]{:S(2)}) copy-start(f32[12,4,8,512]{3,2,1,0:T(8,128)S(1)} %collective-permute-done.9.refs_9_.refs_7_) | copy-start | bytes 2359300
  213.8 123.7 %collective-permute-start.19 = (f32[12,3,8,512]{3,2,1,0:T(8,128)S(1)}, f32[12,3,8,512]{3,2,1,0:T(8,128)}, u32[]{:S(2)}, u32[]{:S(2)}) collective-permute-start(f32[12,3,8,512]{3,2,1,0:T(8,128)S(1)} %get-tuple-element.63), channel_id=1, source_target_pairs={{0,8},{4,12},{8,0},{12,4},{1,9},{5,13},{9,1},{13,5},{2,10},{6,14},... | collective-permute-start | bytes 1769480 | tf_op jit(solution)/shard_map/ppermute | solution.py:281
  213.9 79.2 %copy-start.13 = (f32[12,4,8,512]{3,2,1,0:T(8,128)}, f32[12,4,8,512]{3,2,1,0:T(8,128)S(1)}, u32[]{:S(2)}) copy-start(f32[12,4,8,512]{3,2,1,0:T(8,128)S(1)} %collective-permute-done.11.refs_11_.refs_9_) | copy-start | bytes 2359300
  213.9 123.7 %collective-permute-start.20 = (f32[12,3,8,512]{3,2,1,0:T(8,128)S(1)}, f32[12,3,8,512]{3,2,1,0:T(8,128)}, u32[]{:S(2)}, u32[]{:S(2)}) collective-permute-start(f32[12,3,8,512]{3,2,1,0:T(8,128)S(1)} %get-tuple-element.64), channel_id=1, source_target_pairs={{0,12},{4,0},{8,4},{12,8},{1,13},{5,1},{9,5},{13,9},{2,14},{6,2},{... | collective-permute-start | bytes 1769480 | tf_op jit(solution)/shard_map/ppermute | solution.py:281
  241.8 51.3 %copy-start.17 = (f32[12,4,8,512]{3,2,1,0:T(8,128)}, f32[12,4,8,512]{3,2,1,0:T(8,128)S(1)}, u32[]{:S(2)}) copy-start(f32[12,4,8,512]{3,2,1,0:T(8,128)S(1)} %collective-permute-done.21.refs_5_) | copy-start | bytes 2359300
  241.8 102.3 %collective-permute-start.13 = (f32[12,1,8,512]{3,2,1,0:T(8,128)S(1)}, f32[12,1,8,512]{3,2,1,0:T(8,128)S(1)}, u32[]{:S(2)}, u32[]{:S(2)}) collective-permute-start(f32[12,1,8,512]{3,2,1,0:T(8,128)S(1)} %get-tuple-element.56), channel_id=1, source_target_pairs={{0,4},{4,8},{8,12},{12,0},{1,5},{5,9},{9,13},{13,1},{2,6},{6,10},{... | collective-permute-start | bytes 589832 | tf_op jit(solution)/shard_map/ppermute | solution.py:281
  268.5 24.6 %copy-start.18 = (f32[12,4,8,512]{3,2,1,0:T(8,128)}, f32[12,4,8,512]{3,2,1,0:T(8,128)S(1)}, u32[]{:S(2)}) copy-start(f32[12,4,8,512]{3,2,1,0:T(8,128)S(1)} %collective-permute-done.22.refs_7_) | copy-start | bytes 2359300
  268.5 75.6 %collective-permute-start.15 = (f32[12,1,8,512]{3,2,1,0:T(8,128)S(1)}, f32[12,1,8,512]{3,2,1,0:T(8,128)}, u32[]{:S(2)}, u32[]{:S(2)}) collective-permute-start(f32[12,1,8,512]{3,2,1,0:T(8,128)S(1)} %get-tuple-element.58), channel_id=1, source_target_pairs={{0,8},{4,12},{8,0},{12,4},{1,9},{5,13},{9,1},{13,5},{2,10},{6,14},... | collective-permute-start | bytes 589832 | tf_op jit(solution)/shard_map/ppermute | solution.py:281
  270.4 22.7 %copy-start.19 = (f32[12,4,8,512]{3,2,1,0:T(8,128)}, f32[12,4,8,512]{3,2,1,0:T(8,128)S(1)}, u32[]{:S(2)}) copy-start(f32[12,4,8,512]{3,2,1,0:T(8,128)S(1)} %collective-permute-done.23.refs_9_) | copy-start | bytes 2359300
  270.4 73.7 %collective-permute-start.17 = (f32[12,1,8,512]{3,2,1,0:T(8,128)S(1)}, f32[12,1,8,512]{3,2,1,0:T(8,128)}, u32[]{:S(2)}, u32[]{:S(2)}) collective-permute-start(f32[12,1,8,512]{3,2,1,0:T(8,128)S(1)} %get-tuple-element.60), channel_id=1, source_target_pairs={{0,12},{4,0},{8,4},{12,8},{1,13},{5,1},{9,5},{13,9},{2,14},{6,2},{... | collective-permute-start | bytes 589832 | tf_op jit(solution)/shard_map/ppermute | solution.py:281
  344.1 0.7 copy-start.21

commit v2 on v1

--- a/solution.py
+++ b/solution.py
@@ -20,6 +20,14 @@
 f32 = jnp.float32
 
 
+def cost(us):
+    return pl.CostEstimate(flops=int(us * 1e6), transcendentals=0, bytes_accessed=int(us * 3e3))
+
+
+def tied(values, *earlier):
+    return lax.optimization_barrier((values, earlier))[0]
+
+
 def thirds(x):
     top = x.astype(jnp.bfloat16)
     x = x - top.astype(f32)
@@ -43,48 +51,36 @@
     return product(a, b, ((1,), (0,)))
 
 
-def pack_kernel(*refs, members, two, statics):
+def pack_kernel(*refs, chunk, two, statics, waits):
     ens_head, ens_tail, ens_first, ens_last, ens_hf, ens_hl, ens_tf, ens_tl = refs[:8]
-    refs = refs[8:]
-    if statics:
-        thick, wet = refs[:2]
-        refs = refs[2:]
-    outs = refs
+    outs = refs[8 + (2 if statics else 0) + waits :]
     b, s = lax.axis_index("blk"), lax.axis_index("sub")
-    step = pl.program_id(0)
-
-    def emit(head, tail, first, last, corner_head, corner_tail, index):
+
+    def emit(head, tail, first, last, corner_head, corner_tail, i, index):
         if two:
-            outs[0][0, index] = jnp.where(b == 0, tail, head)
-            outs[1][0, index] = jnp.where(b == 0, corner_tail, corner_head)
+            outs[0][i, index] = jnp.where(b == 0, tail, head)
+            outs[1][i, index] = jnp.where(b == 0, corner_tail, corner_head)
         else:
-            outs[0][0, index] = head
-            outs[1][0, index] = corner_head
-            outs[2][0, index] = tail
-            outs[3][0, index] = corner_tail
-        outs[-1][0, index] = jnp.where(s == 0, last, first)
-
-    def member():
+            outs[0][i, index] = head
+            outs[1][i, index] = corner_head
+            outs[2][i, index] = tail
+            outs[3][i, index] = corner_tail
+        outs[-1][i, index] = jnp.where(s == 0, last, first)
+
+    for i in range(chunk):
         for field in range(3):
             emit(
-                ens_head[0, field, :HALO],
-                ens_tail[0, field, PAD - HALO :],
-                ens_first[0, field],
-                ens_last[0, field],
-                jnp.where(s == 0, ens_hl[0, field, :HALO], ens_hf[0, field, :HALO]),
-                jnp.where(s == 0, ens_tl[0, field, PAD - HALO :], ens_tf[0, field, PAD - HALO :]),
+                ens_head[i, field, :HALO],
+                ens_tail[i, field, PAD - HALO :],
+                ens_first[i, field],
+                ens_last[i, field],
+                jnp.where(s == 0, ens_hl[i, field, :HALO], ens_hf[i, field, :HALO]),
+                jnp.where(s == 0, ens_tl[i, field, PAD - HALO :], ens_tf[i, field, PAD - HALO :]),
+                i,
                 field,
             )
-
-    if not statics:
-        member()
-        return
-
-    pl.when(step < members)(member)
-
-    @pl.when(step == members)
-    def _():
-        for index, source in enumerate((thick[...], wet[...].astype(f32))):
+    if statics:
+        for index, source in enumerate((refs[8][...], refs[9][...].astype(f32))):
             rows, columns = source.shape
             head, tail = source[:HALO], source[rows - HALO :]
             first, last = source[:, :LANES], source[:, columns - LANES :]
@@ -95,18 +91,21 @@
                 last,
                 jnp.where(s == 0, head[:, columns - LANES :], head[:, :LANES]),
                 jnp.where(s == 0, tail[:, columns - LANES :], tail[:, :LANES]),
+                chunk,
                 index,
             )
 
 
-def edges(ensemble, first, members, statics):
+def edges(ensemble, first, members, statics, after):
     rows, columns = ensemble.shape[2:]
     two = lax.axis_size("blk") == 2
+    chunk = math.gcd(first, members) if not statics else members
     held = members + (1 if statics else 0)
+    block = chunk + (1 if statics else 0)
     row_end, column_end = rows // PAD - 1, columns // LANES - 1
 
-    def taken(block, r, c):
-        return pl.BlockSpec((1, 3) + block, lambda i: (first + jnp.minimum(i, members - 1), 0, r, c))
+    def taken(shape, r, c):
+        return pl.BlockSpec((chunk, 3) + shape, lambda i: (first // chunk + i, 0, r, c))
 
     in_specs = [
         taken((PAD, columns), 0, 0),
@@ -118,19 +117,18 @@
         taken((PAD, LANES), row_end, 0),
         taken((PAD, LANES), row_end, column_end),
     ]
-    operands = [ensemble] * 8
-    if statics:
-        in_specs += [pl.BlockSpec((rows, columns), lambda i: (0, 0))] * 2
-        operands += list(statics)
+    in_specs += [pl.BlockSpec((rows, columns), lambda i: (0, 0))] * len(statics)
+    in_specs += [pl.BlockSpec(memory_space=pl.ANY)] * len(after)
     shapes = [(3, HALO, columns), (3, HALO, LANES)] * (1 if two else 2) + [(3, rows, LANES)]
     packed = pl.pallas_call(
-        functools.partial(pack_kernel, members=members, two=two, statics=bool(statics)),
-        grid=(held,),
+        functools.partial(pack_kernel, chunk=chunk, two=two, statics=bool(statics), waits=len(after)),
+        grid=(members // chunk,),
         in_specs=in_specs,
-        out_specs=[pl.BlockSpec((1,) + s, lambda i: (i, 0, 0, 0)) for s in shapes],
+        out_specs=[pl.BlockSpec((block,) + s, lambda i: (i, 0, 0, 0)) for s in shapes],
         out_shape=[jax.ShapeDtypeStruct((held,) + s, f32) for s in shapes],
+        cost_estimate=cost(3),
         name="edges",
-    )(*operands)
+    )(*[ensemble] * 8, *statics, *after)
     return halo(packed)
 
 
@@ -250,7 +248,7 @@
                 out[0, q - start] = res[field, domain, piece * size : (piece + 1) * size]
 
 
-def forecast(ensemble, first, members, fields, mem_halo, sta_halo, static_at, size, ranges):
+def forecast(ensemble, first, members, fields, mem_halo, halo_first, sta_halo, static_at, size, ranges):
     thick, wet = fields
     rows, columns = ensemble.shape[2:]
     parts, tiles = lax.axis_size("grid"), lax.axis_size("blk")
@@ -258,7 +256,7 @@
     ext = pltpu.VMEM((rows + 2 * PAD, columns + LANES), f32)
     whole = pl.BlockSpec((rows, columns), lambda i: (0, 0))
     in_specs = [pl.BlockSpec((1, 3, rows, columns), lambda i: (first + i, 0, 0, 0)), whole, whole]
-    in_specs += [pl.BlockSpec((1,) + x.shape[1:], lambda i: (i, 0, 0, 0)) for x in mem_halo]
+    in_specs += [pl.BlockSpec((1,) + x.shape[1:], lambda i: (halo_first + i, 0, 0, 0)) for x in mem_halo]
     in_specs += [pl.BlockSpec((1,) + x.shape[1:], lambda i: (static_at, 0, 0, 0)) for x in sta_halo]
     shapes = [(stop - start, size, columns) for start, stop in ranges for shift in range(parts)]
     flat = pl.pallas_call(
@@ -269,6 +267,7 @@
         out_shape=[jax.ShapeDtypeStruct((members,) + s, f32) for s in shapes],
         scratch_shapes=[ext] * 10 + [pltpu.VMEM((3, parts, lines, columns), f32)],
         compiler_params=pltpu.CompilerParams(vmem_limit_bytes=48 << 20),
+        cost_estimate=cost(3 * members),
         name="forecast",
     )(ensemble, thick, wet, *mem_halo, *sta_halo)
     return [flat[i * parts : (i + 1) * parts] for i in range(len(ranges))]
@@ -341,6 +340,7 @@
         out_specs=pl.BlockSpec((members + PAD, members), lambda q: (0, 0)),
         out_shape=jax.ShapeDtypeStruct((members + PAD, members), f32),
         scratch_shapes=[pltpu.VMEM((members, slots), f32)],
+        cost_estimate=cost(6),
         name="observe",
     )(count.reshape(1, 1), cell.reshape(1, slots), value.reshape(1, slots), error.reshape(1, slots), *pieces)
 
@@ -405,6 +405,7 @@
     return pl.pallas_call(
         functools.partial(transform_kernel, parts=parts, members=members),
         out_shape=[shape, shape],
+        cost_estimate=cost(12),
         name="transform",
     )(packed)
 
@@ -436,6 +437,7 @@
         out_specs=pl.BlockSpec((shape[0], 1) + shape[2:], lambda q: (0, q + q0, 0, 0)),
         out_shape=jax.ShapeDtypeStruct(shape, f32),
         input_output_aliases=aliases,
+        cost_estimate=cost(2 * (q1 - q0)),
         name="analysis",
     )(*operands)
 
@@ -449,37 +451,39 @@
     per_field = lines // size
     total = 3 * per_field
     width = size * columns // PAD
-    early = max(1, held // 4)
-    late = held - early
+    first, early = max(1, held // 16), max(1, held // 4)
     fields = (basin_thickness, wet_indicator)
-    halo_early = edges(ensemble, 0, early, fields)
-    halo_late = edges(ensemble, early, late, ())
-    ranges_early = [(0, per_field), (per_field, total)]
     cuts = sorted({0, per_field, 2 * per_field, total - 1, total})
-    ranges_late = list(zip(cuts[:-1], cuts[1:]))
-    sent_early = forecast(ensemble, 0, early, fields, halo_early, halo_early, early, size, ranges_early)
-    sent_late = forecast(ensemble, early, late, fields, halo_late, halo_early, early, size, ranges_late)
+    ranges = list(zip(cuts[:-1], cuts[1:]))
 
     def received(pieces):
         got = exchange(pieces)
         return [x.reshape(x.shape[0], x.shape[1], PAD, width) for x in got]
 
-    early_h = received(sent_early[0])
-    late_h = received(sent_late[0])
-    early_uv = received(sent_early[1])
-    late_uv = [received(x) for x in sent_late[1:]]
-
-    def woven(a, b):
-        return [x for pair in zip(a, b) for x in pair]
-
-    packed = observe(woven(early_h, late_h), per_field, members, obs_cell, obs_count, obs_value, obs_error)
+    halo_early = edges(ensemble, 0, early, fields, ())
+    groups, starts = [], []
+    for start, stop in [(0, first)] + ([(first, early)] if early > first else []):
+        (sent,) = forecast(ensemble, start, stop - start, fields, halo_early, start, halo_early, early, size, [(0, total)])
+        groups.append(sent)
+    halo_late = edges(ensemble, early, held - early, (), (groups[0][0],))
+    whole = [received(sent) for sent in groups]
+    halo_late = tied(halo_late, whole[0])
+    sent_late = forecast(ensemble, early, held - early, fields, halo_late, 0, halo_early, early, size, ranges)
+    late = [received(sent_late[0]), received(tied(sent_late[1], whole[-1]))]
+    late.append(received(tied(sent_late[2], late[0])))
+
+    def woven(pieces, offset):
+        return [x for per_source in zip(*whole, pieces) for x in per_source], ([offset] * len(whole) + [0]) * parts
+
+    heights, at = woven(late[0], 0)
+    packed = observe(heights, per_field, members, obs_cell, obs_count, obs_value, obs_error)
     packed = lax.psum(packed, ("blk", "sub"))
     mixers = transform(packed, members)
+    late += [received(tied(x, late[1], mixers)) for x in sent_late[3:]]
     shape = (members, total, PAD, width)
-    out = analyse(mixers, woven(early_h, late_h), [0] * (2 * parts), 0, per_field, shape, None)
-    for (start, stop), pieces in zip(ranges_late[1:], late_uv):
-        offset = [start - per_field, 0] * parts
-        out = analyse(mixers, woven(early_uv, pieces), offset, start, stop, shape, out)
+    out = None
+    for (start, stop), pieces in zip(ranges, late):
+        out = analyse(mixers, *woven(pieces, start), start, stop, shape, out)
     return out.reshape(members, 3, 1, lines, columns)
 
 

time: 349 us -> 317 us (0.908)
  starting transfers between devices: 147 us -> 120 us
  waiting for transfers between devices: 77.6 us -> 55.1 us
  blocking collectives: 11.8 us -> 31.4 us
  Pallas kernels: 106 us -> 102 us
    ppermute x18, starting transfers between devices: 141 us -> 115 us  [exchange(): lax.ppermute(pieces[shift], 'grid', [(i, (i + shift) % parts) for i in ra...]
    ppermute x18, waiting for transfers between devices: 67.4 us -> 47.8 us  [exchange(): lax.ppermute(pieces[shift], 'grid', [(i, (i + shift) % parts) for i in ra...]
    psum x1, blocking collectives: 11.8 us -> 31.4 us  [shards(): packed = lax.psum(packed, ('blk', 'sub'))]
    ppermute x2, waiting for transfers between devices: 10.1 us -> 4.53 us  [halo(): lax.ppermute(packed[1], ('blk', 'sub'), [(0, 3), (3, 0), (1, 2), (2, 1)])]
    pallas_call x2, Pallas kernels: 12.8 us -> 7.98 us  [edges(): pl.pallas_call(functools.partial(pack_kernel, chunk=chunk, two=two, stati...]
    pallas_call x2 -> x3, Pallas kernels: 50.5 us -> 51.4 us  [forecast(): pl.pallas_call(functools.partial(forecast_kernel, parts=parts, tiles=tile...]
  transfers between devices with their start and end apart: 24 -> 24, of which waited for: 5 -> 3; matrix products, arithmetic and copies ran while one was open for 0% -> 0% of each run, Pallas kernels for 27% -> 27%
where the time goes in v2:
time: 317 us
  starting transfers between devices  120 us (38%)
  Pallas kernels  102 us (32%)
  waiting for transfers between devices  55.1 us (17%)
  blocking collectives  31.4 us (10%)
  local copies, waits for them, and re-layouts  6.76 us (2%)
    ppermute x18, starting transfers between devices, exchange(): lax.ppermute(pieces[shift], 'grid', [(i, (i + shift) % parts) for i in ra...  115 us
    pallas_call x3, Pallas kernels, forecast(): pl.pallas_call(functools.partial(forecast_kernel, parts=parts, tiles=tile...  51.4 us
    ppermute x18, waiting for transfers between devices, exchange(): lax.ppermute(pieces[shift], 'grid', [(i, (i + shift) % parts) for i in ra...  47.8 us
    psum x1, blocking collectives, shards(): packed = lax.psum(packed, ('blk', 'sub'))  31.4 us
    pallas_call x4, Pallas kernels, analyse(): pl.pallas_call(functools.partial(analysis_kernel, carried=int(carried is...  25 us
    pallas_call x1, Pallas kernels, transform(): pl.pallas_call(functools.partial(transform_kernel, parts=parts, members=m...  12.2 us
    pallas_call x2, Pallas kernels, edges(): pl.pallas_call(functools.partial(pack_kernel, chunk=chunk, two=two, stati...  7.98 us
    unnamed x48, local copies, waits for them, and re-layouts  6.76 us
  transfers between devices with their start and end apart: 24, of which 3 were waited for; matrix products, arithmetic and copies ran while one was open for 0% of the time, Pallas kernels for 27%

profile of v2, /device:TPU:0, one launch (start us, length us, event | category | flops | bytes accessed | tf_op | source)
XLA Modules:
  0.0 316.7 jit_solution(4429421890241562470)
XLA Ops:
  0.0 2.9 edges.2
  2.9 0.5 collective-permute-start.1
  3.4 2.5 collective-permute-start
  5.9 0.1 collective-permute-start.2
  6.0 4.5 %collective-permute-done.2.refs_6_.refs_7_.refs_11_.refs_12_ = f32[5,3,4,128]{3,2,1,0:T(4,128)S(1)} collective-permute-done((f32[5,3,4,128]{3,2,1,0:T(4,128)}, f32[5,3,4,128]{3,2,1,0:T(4,128)S(1)}, u32[]{:S(2)}, u32[]{:S(2)}) %collective-permute-start.2) | collective-permute-done | bytes 30752 | tf_op jit(solution)/shard_map/ppermute | solution.py:140
  10.5 0.0 collective-permute-done.refs_3_.refs_4_.refs_8_.refs_9_
  10.5 0.0 collective-permute-done.1.refs_5_.refs_10_
  10.6 4.3 %forecast.3 = (f32[1,12,8,512]{3,2,1,0:T(8,128)S(1)}, f32[1,12,8,512]{3,2,1,0:T(8,128)S(1)}, f32[1,12,8,512]{3,2,1,0:T(8,128)S(1)}, f32[1,12,8,512]{3,2,1,0:T(8,128)S(1)}) custom-call(f32[16,3,128,512]{3,2,1,0:T(8,128)} %refs_0_.9, f32[128,512]{1,0:T(8,128)S(1)} %copy-done.3, s32[128,512]{1,0:T(8,128)S(1)} %copy-done.4, ...), custom_call_target="tpu_custom_call" | custom-call | flops 3000000 | bytes 9000 | tf_op jit(solution)/shard_map/forecast/pallas_call | solution.py:262
  14.8 0.7 copy-done.2
  15.5 5.1 %edges.3 = (f32[12,3,4,512]{3,2,1,0:T(4,128)}, f32[12,3,4,128]{3,2,1,0:T(4,128)}, f32[12,3,128,128]{3,2,1,0:T(8,128)}) custom-call(f32[16,3,128,512]{3,2,1,0:T(8,128)} %refs_0_.9, f32[16,3,128,512]{3,2,1,0:T(8,128)} %refs_0_.9, f32[16,3,128,512]{3,2,1,0:T(8,128)} %refs_0_.9, f32[16,3,128,512]{3,2,1,0:T(8,128)} %refs_0_.9, f32[16,3,128,512]{3,2,1,0:T(8,128)} %refs_0_.9, ...), custom_call_target="tpu_custom_call" | custom-call | flops 3000000 | bytes 9000 | tf_op jit(solution)/shard_map/edges/pallas_call | solution.py:123
  20.6 0.2 collective-permute-start.4
  20.8 1.7 collective-permute-start.6
  22.5 1.2 collective-permute-start.5
  23.6 2.6 collective-permute-start.7
  26.2 1.3 collective-permute-start.8
  27.6 10.0 %forecast.4 = (f32[3,12,8,512]{3,2,1,0:T(8,128)S(1)}, f32[3,12,8,512]{3,2,1,0:T(8,128)S(1)}, f32[3,12,8,512]{3,2,1,0:T(8,128)S(1)}, f32[3,12,8,512]{3,2,1,0:T(8,128)S(1)}) custom-call(f32[16,3,128,512]{3,2,1,0:T(8,128)} %refs_0_.9, f32[128,512]{1,0:T(8,128)S(1)} %copy-done.3, s32[128,512]{1,0:T(8,128)S(1)} %copy-done.4, ...), custom_call_target="tpu_custom_call" | custom-call | flops 9000000 | bytes 27000 | tf_op jit(solution)/shard_map/forecast/pallas_call | solution.py:262
  37.6 0.9 copy-done.1
  38.4 0.0 collective-permute-done.5.refs_6_.refs_7_
  38.5 0.7 collective-permute-start.9
  39.1 0.0 collective-permute-done.6.refs_7_.refs_5_
  39.1 0.6 collective-permute-start.3
  39.7 0.0 collective-permute-done.7.refs_10_.refs_8_
  39.8 1.4 collective-permute-start.11
  41.1 0.0 collective-permute-done.8.refs_13_.refs_11_
  41.1 3.7 %collective-permute-start.13 = (f32[3,12,8,512]{3,2,1,0:T(8,128)S(1)}, f32[3,12,8,512]{3,2,1,0:T(8,128)S(1)}, u32[]{:S(2)}, u32[]{:S(2)}) collective-permute-start(f32[3,12,8,512]{3,2,1,0:T(8,128)S(1)} %get-tuple-element.75), channel_id=1, source_target_pairs={{0,12},{4,0},{8,4},{12,8},{1,13},{5,1},{9,5},{13,9},{2,14},{6,2},{... | collective-permute-start | bytes 1769480 | tf_op jit(solution)/shard_map/ppermute | solution.py:280
  44.9 2.9 collective-permute-done.3.refs_3_.refs_4_
  47.7 0.0 collective-permute-done.4.refs_5_
  47.7 1.4 copy-done.17
  49.1 37.2 %forecast.5 = (f32[12,4,8,512]{3,2,1,0:T(8,128)S(1)}, f32[12,4,8,512]{3,2,1,0:T(8,128)S(1)}, f32[12,4,8,512]{3,2,1,0:T(8,128)}, f32[12,4,8,512]{3,2,1,0:T(8,128)...) custom-call(f32[16,3,128,512]{3,2,1,0:T(8,128)} %refs_0_.9, ...), custom_call_target="tpu_custom_call" | custom-call | flops 36000000 | bytes 108000 | tf_op jit(solution)/shard_map/forecast/pallas_call | solution.py:262
  86.3 0.9 copy-done.5
  87.2 0.8 copy-done.6
  88.0 0.7 copy-done.7
  88.7 0.3 collective-permute-start.10
  89.0 3.5 %collective-permute-start.12 = (f32[12,4,8,512]{3,2,1,0:T(8,128)}, f32[12,4,8,512]{3,2,1,0:T(8,128)S(1)}, u32[]{:S(2)}, u32[]{:S(2)}) collective-permute-start(f32[12,4,8,512]{3,2,1,0:T(8,128)} %get-tuple-element.74), channel_id=1, source_target_pairs={{0,8},{4,12},{8,0},{12,4},{1,9},{5,13},{9,1},{13,5},{2,10},{6,14},... | collective-permute-start | bytes 2359304 | tf_op jit(solution)/shard_map/ppermute | solution.py:280
  92.5 0.0 collective-permute-done.9.refs_8_.refs_6_
  92.5 0.1 collective-permute-start.14
  92.6 0.0 collective-permute-done.11.refs_11_.refs_9_
  92.6 0.0 collective-permute-done.13.refs_14_.refs_12_
  92.6 34.3 %collective-permute-start.15 = (f32[12,4,8,512]{3,2,1,0:T(8,128)}, f32[12,4,8,512]{3,2,1,0:T(8,128)S(1)}, u32[]{:S(2)}, u32[]{:S(2)}) collective-permute-start(f32[12,4,8,512]{3,2,1,0:T(8,128)} %get-tuple-element.88), channel_id=1, source_target_pairs={{0,4},{4,8},{8,12},{12,0},{1,5},{5,9},{9,13},{13,1},{2,6},{6,10},{... | collective-permute-start | bytes 2359304 | tf_op jit(solution)/shard_map/ppermute | solution.py:280
  126.9 0.0 collective-permute-start.16
  127.0 0.0 collective-permute-done.10.refs_9_.refs_7_
  127.0 2.4 collective-permute-start.17
  129.3 47.7 %collective-permute-done.12.refs_12_.refs_10_ = f32[12,4,8,512]{3,2,1,0:T(8,128)S(1)} collective-permute-done((f32[12,4,8,512]{3,2,1,0:T(8,128)}, f32[12,4,8,512]{3,2,1,0:T(8,128)S(1)}, u32[]{:S(2)}, u32[]{:S(2)}) %collective-permute-start.12) | collective-permute-done | bytes 786464 | tf_op jit(solution)/shard_map/ppermute | solution.py:280
  177.0 0.0 collective-permute-done.14.refs_15_.refs_13_
  177.0 18.1 %collective-permute-start.21 = (f32[12,3,8,512]{3,2,1,0:T(8,128)S(1)}, f32[12,3,8,512]{3,2,1,0:T(8,128)S(1)}, u32[]{:S(2)}, u32[]{:S(2)}) collective-permute-start(f32[12,3,8,512]{3,2,1,0:T(8,128)S(1)} %get-tuple-element.100), channel_id=1, source_target_pairs={{0,4},{4,8},{8,12},{12,0},{1,5},{5,9},{9,13},{13,1},{2,6},{6,10},{... | collective-permute-start | bytes 1769480 | tf_op jit(solution)/shard_map/ppermute | solution.py:280
  195.2 1.9 collective-permute-start.22
  197.1 0.4 collective-permute-start.23
  198.3 5.5 %observe.1 = f32[72,64]{1,0:T(8,128)} custom-call(s32[1,1]{1,0:T(1,128)} %bitcast.7.refs_0_, s32[1,64]{1,0:T(1,128)} %bitcast.8, f32[1,64]{1,0:T(1,128)} %bitcast.9, f32[1,64]{1,0:T(1,128)} %bitcast.10, f32[1,12,8,512]{3,2,1,0:T(8,128)} %copy-done.2, f32[3,12,8,512]{3,2,1,0:T(8,128)} %copy-done.1, f32[12,4,8,512]{3,2,1,0:T(8,128)} %copy-done.5, ...), custom_call_target="tpu_custom_call" | custom-call | flops 6000000 | bytes 18000 | tf_op jit(solution)/shard_map/observe/pallas_call | solution.py:336
  203.8 31.4 %psum.7.packed = f32[72,64]{1,0:T(8,128)} all-reduce(f32[72,64]{1,0:T(8,128)} %observe.1), channel_id=1, replica_groups=mesh['copy'=2,'grid'=4,'blk'=2,'sub'=2] {'blk','sub'}, use_global_device_ids=true, to_apply=%region_0.0 | all-reduce | flops 4608 | bytes 36864 | tf_op jit(solution)/shard_map/psum | solution.py:480
  235.2 12.2 %transform.1 = (bf16[512,512]{1,0:T(8,128)(2,1)}, bf16[512,512]{1,0:T(8,128)(2,1)}) custom-call(f32[72,64]{1,0:T(8,128)} %psum.7.packed), custom_call_target="tpu_custom_call" | custom-call | flops 12000000 | bytes 36000 | tf_op jit(solution)/shard_map/transform/pallas_call | solution.py:405
  247.4 38.8 %collective-permute-start.18 = (f32[12,1,8,512]{3,2,1,0:T(8,128)S(1)}, f32[12,1,8,512]{3,2,1,0:T(8,128)S(1)}, u32[]{:S(2)}, u32[]{:S(2)}) collective-permute-start(f32[12,1,8,512]{3,2,1,0:T(8,128)S(1)} %get-tuple-element.92), channel_id=1, source_target_pairs={{0,4},{4,8},{8,12},{12,0},{1,5},{5,9},{9,13},{13,1},{2,6},{6,10},{... | collective-permute-start | bytes 589832 | tf_op jit(solution)/shard_map/ppermute | solution.py:280
  286.2 3.7 %collective-permute-start.19 = (f32[12,1,8,512]{3,2,1,0:T(8,128)S(1)}, f32[12,1,8,512]{3,2,1,0:T(8,128)S(1)}, u32[]{:S(2)}, u32[]{:S(2)}) collective-permute-start(f32[12,1,8,512]{3,2,1,0:T(8,128)S(1)} %get-tuple-element.93), channel_id=1, source_target_pairs={{0,8},{4,12},{8,0},{12,4},{1,9},{5,13},{9,1},{13,5},{2,10},{6,14},... | collective-permute-start | bytes 589832 | tf_op jit(solution)/shard_map/ppermute | solution.py:280
  289.9 0.3 collective-permute-start.20
  290.3 7.5 %analysis.4.refs_14_ = f32[64,12,8,512]{3,2,1,0:T(8,128)} custom-call(bf16[512,512]{1,0:T(8,128)(2,1)} %get-tuple-element.77.refs_0_, bf16[512,512]{1,0:T(8,128)(2,1)} %get-tuple-element.78.refs_1_, f32[1,12,8,512]{3,2,1,0:T(8,128)} %copy-done.2, f32[3,12,8,512]{3,2,1,0:T(8,128)} %copy-done.1, f32[12,4,8,512]{3,2,1,0:T(8,128)} %copy-done.5, ...), custom_call_target="tpu_custom_call" | custom-call | flops 8000000 | bytes 24000 | tf_op jit(solution)/shard_map/analysis/pallas_call | solution.py:433
  297.7 7.5 %analysis.5.refs_14_ = f32[64,12,8,512]{3,2,1,0:T(8,128)} custom-call(bf16[512,512]{1,0:T(8,128)(2,1)} %get-tuple-element.77.refs_0_, bf16[512,512]{1,0:T(8,128)(2,1)} %get-tuple-element.78.refs_1_, f32[1,12,8,512]{3,2,1,0:T(8,128)} %copy-done.2, f32[3,12,8,512]{3,2,1,0:T(8,128)} %copy-done.1, ...), custom_call_target="tpu_custom_call", output_to_operand_aliasing={{}: (14, {})} | custom-call | flops 8000000 | bytes 24000 | tf_op jit(solution)/shard_map/analysis/pallas_call | solution.py:433
  305.3 0.0 collective-permute-done.22.refs_10_
  305.3 0.0 collective-permute-done.23.refs_13_
  305.3 6.5 %analysis.6.refs_14_ = f32[64,12,8,512]{3,2,1,0:T(8,128)} custom-call(bf16[512,512]{1,0:T(8,128)(2,1)} %get-tuple-element.77.refs_0_, bf16[512,512]{1,0:T(8,128)(2,1)} %get-tuple-element.78.refs_1_, f32[1,12,8,512]{3,2,1,0:T(8,128)} %copy-done.2, f32[3,12,8,512]{3,2,1,0:T(8,128)} %copy-done.1, ...), custom_call_target="tpu_custom_call", output_to_operand_aliasing={{}: (14, {})} | custom-call | flops 6000000 | bytes 18000 | tf_op jit(solution)/shard_map/analysis/pallas_call | solution.py:433
  311.8 0.0 collective-permute-done.18.refs_7_
  311.8 0.0 collective-permute-done.20.refs_13_
  311.8 0.6 copy-done.20
  312.5 0.1 copy-done.21
  312.5 0.7 copy-done.22
  313.2 3.5 %analysis.7 = f32[64,12,8,512]{3,2,1,0:T(8,128)} custom-call(bf16[512,512]{1,0:T(8,128)(2,1)} %get-tuple-element.77.refs_0_, bf16[512,512]{1,0:T(8,128)(2,1)} %get-tuple-element.78.refs_1_, f32[1,12,8,512]{3,2,1,0:T(8,128)} %copy-done.2, f32[3,12,8,512]{3,2,1,0:T(8,128)} %copy-done.1, f32[12,1,8,512]{3,2,1,0:T(8,128)} %copy-done.7, ...), custom_call_target="tpu_custom_call", output_to_operand_aliasing={{}: (14, {})} | custom-call | flops 2000000 | bytes 6000 | tf_op jit(solution)/shard_map/analysis/pallas_call | solution.py:433
  (44 shorter events, 0.1 us)
Async XLA Ops:
  0.0 10.5 %copy-start.4 = (s32[128,512]{1,0:T(8,128)S(1)}, s32[128,512]{1,0:T(8,128)}, u32[]{:S(2)}) copy-start(s32[128,512]{1,0:T(8,128)} %refs_2_.9) | copy-start | bytes 786436
  0.0 10.5 %copy-start.3 = (f32[128,512]{1,0:T(8,128)S(1)}, f32[128,512]{1,0:T(8,128)}, u32[]{:S(2)}) copy-start(f32[128,512]{1,0:T(8,128)} %refs_1_.9) | copy-start | bytes 786436
  2.9 7.6 %collective-permute-start.1 = (f32[5,3,128,128]{3,2,1,0:T(8,128)}, f32[5,3,128,128]{3,2,1,0:T(8,128)S(1)}, u32[]{:S(2)}, u32[]{:S(2)}) collective-permute-start(f32[5,3,128,128]{3,2,1,0:T(8,128)} %get-tuple-element.55), channel_id=1, source_target_pairs={{0,1},{1,0},{2,3},{3,2},{4,5},{5,4},{6,7},{7,6},{8,9},{9,8},{10,11... | collective-permute-start | bytes 2949128 | tf_op jit(solution)/shard_map/ppermute | solution.py:137
  3.4 7.2 %collective-permute-start = (f32[5,3,4,512]{3,2,1,0:T(4,128)}, f32[5,3,4,512]{3,2,1,0:T(4,128)S(1)}, u32[]{:S(2)}, u32[]{:S(2)}) collective-permute-start(f32[5,3,4,512]{3,2,1,0:T(4,128)} %get-tuple-element.54), channel_id=1, source_target_pairs={{0,2},{2,0},{1,3},{3,1},{4,6},{6,4},{5,7},{7,5},{8,10},{10,8},{9,1... | collective-permute-start | bytes 368648 | tf_op jit(solution)/shard_map/ppermute | solution.py:139
  5.9 4.7 %collective-permute-start.2 = (f32[5,3,4,128]{3,2,1,0:T(4,128)}, f32[5,3,4,128]{3,2,1,0:T(4,128)S(1)}, u32[]{:S(2)}, u32[]{:S(2)}) collective-permute-start(f32[5,3,4,128]{3,2,1,0:T(4,128)} %get-tuple-element.56), channel_id=1, source_target_pairs={{0,3},{3,0},{1,2},{2,1},{4,7},{7,4},{5,6},{6,5},{8,11},{11,8},{9,1... | collective-permute-start | bytes 92168 | tf_op jit(solution)/shard_map/ppermute | solution.py:140
  10.6 17.0 %copy-start = (f32[5,3,128,128]{3,2,1,0:T(8,128)}, f32[5,3,128,128]{3,2,1,0:T(8,128)S(1)}, u32[]{:S(2)}) copy-start(f32[5,3,128,128]{3,2,1,0:T(8,128)S(1)} %collective-permute-done.1.refs_5_.refs_10_) | copy-start | bytes 2949124
  14.8 0.7 copy-start.2
  20.6 18.6 %copy-start.23 = (f32[12,3,4,512]{3,2,1,0:T(4,128)S(1)}, f32[12,3,4,512]{3,2,1,0:T(4,128)}, u32[]{:S(2)}) copy-start(f32[12,3,4,512]{3,2,1,0:T(4,128)} %get-tuple-element.59) | copy-start | bytes 884740
  20.6 27.2 %collective-permute-start.4 = (f32[12,3,128,128]{3,2,1,0:T(8,128)}, f32[12,3,128,128]{3,2,1,0:T(8,128)S(1)}, u32[]{:S(2)}, u32[]{:S(2)}) collective-permute-start(f32[12,3,128,128]{3,2,1,0:T(8,128)} %get-tuple-element.60), channel_id=1, source_target_pairs={{0,1},{1,0},{2,3},{3,2},{4,5},{5,4},{6,7},{7,6},{8,9},{9,8},{10,11... | collective-permute-start | bytes 7077896 | tf_op jit(solution)/shard_map/ppermute | solution.py:137
  20.8 18.4 %collective-permute-start.6 = (f32[1,12,8,512]{3,2,1,0:T(8,128)S(1)}, f32[1,12,8,512]{3,2,1,0:T(8,128)S(1)}, u32[]{:S(2)}, u32[]{:S(2)}) collective-permute-start(f32[1,12,8,512]{3,2,1,0:T(8,128)S(1)} %get-tuple-element.62), channel_id=1, source_target_pairs={{0,4},{4,8},{8,12},{12,0},{1,5},{5,9},{9,13},{13,1},{2,6},{6,10},{... | collective-permute-start | bytes 589832 | tf_op jit(solution)/shard_map/ppermute | solution.py:280
  22.5 16.0 %collective-permute-start.5 = (f32[12,3,4,128]{3,2,1,0:T(4,128)}, f32[12,3,4,128]{3,2,1,0:T(4,128)S(1)}, u32[]{:S(2)}, u32[]{:S(2)}) collective-permute-start(f32[12,3,4,128]{3,2,1,0:T(4,128)} %get-tuple-element.61), channel_id=1, source_target_pairs={{0,3},{3,0},{1,2},{2,1},{4,7},{7,4},{5,6},{6,5},{8,11},{11,8},{9,1... | collective-permute-start | bytes 221192 | tf_op jit(solution)/shard_map/ppermute | solution.py:140
  23.6 16.1 %collective-permute-start.7 = (f32[1,12,8,512]{3,2,1,0:T(8,128)S(1)}, f32[1,12,8,512]{3,2,1,0:T(8,128)S(1)}, u32[]{:S(2)}, u32[]{:S(2)}) collective-permute-start(f32[1,12,8,512]{3,2,1,0:T(8,128)S(1)} %get-tuple-element.63), channel_id=1, source_target_pairs={{0,8},{4,12},{8,0},{12,4},{1,9},{5,13},{9,1},{13,5},{2,10},{6,14},... | collective-permute-start | bytes 589832 | tf_op jit(solution)/shard_map/ppermute | solution.py:280
  26.2 14.9 %collective-permute-start.8 = (f32[1,12,8,512]{3,2,1,0:T(8,128)S(1)}, f32[1,12,8,512]{3,2,1,0:T(8,128)S(1)}, u32[]{:S(2)}, u32[]{:S(2)}) collective-permute-start(f32[1,12,8,512]{3,2,1,0:T(8,128)S(1)} %get-tuple-element.64), channel_id=1, source_target_pairs={{0,12},{4,0},{8,4},{12,8},{1,13},{5,1},{9,5},{13,9},{2,14},{6,2},{... | collective-permute-start | bytes 589832 | tf_op jit(solution)/shard_map/ppermute | solution.py:280
  37.6 0.9 copy-start.1
  38.5 54.1 %collective-permute-start.9 = (f32[3,12,8,512]{3,2,1,0:T(8,128)S(1)}, f32[3,12,8,512]{3,2,1,0:T(8,128)S(1)}, u32[]{:S(2)}, u32[]{:S(2)}) collective-permute-start(f32[3,12,8,512]{3,2,1,0:T(8,128)S(1)} %get-tuple-element.71), channel_id=1, source_target_pairs={{0,4},{4,8},{8,12},{12,0},{1,5},{5,9},{9,13},{13,1},{2,6},{6,10},{... | collective-permute-start | bytes 1769480 | tf_op jit(solution)/shard_map/ppermute | solution.py:280
  39.1 159.1 %copy-start.11 = (f32[1,12,8,512]{3,2,1,0:T(8,128)}, f32[1,12,8,512]{3,2,1,0:T(8,128)S(1)}, u32[]{:S(2)}) copy-start(f32[1,12,8,512]{3,2,1,0:T(8,128)S(1)} %collective-permute-done.6.refs_7_.refs_5_) | copy-start | bytes 589828
  39.1 8.6 %collective-permute-start.3 = (f32[12,3,4,512]{3,2,1,0:T(4,128)S(1)}, f32[12,3,4,512]{3,2,1,0:T(4,128)S(1)}, u32[]{:S(2)}, u32[]{:S(2)}) collective-permute-start(f32[12,3,4,512]{3,2,1,0:T(4,128)S(1)} %copy-done.23), channel_id=1, source_target_pairs={{0,2},{2,0},{1,3},{3,1},{4,6},{6,4},{5,7},{7,5},{8,10},{10,8},{9,1... | collective-permute-start | bytes 884744 | tf_op jit(solution)/shard_map/ppermute | solution.py:139
  39.7 158.5 %copy-start.12 = (f32[1,12,8,512]{3,2,1,0:T(8,128)}, f32[1,12,8,512]{3,2,1,0:T(8,128)S(1)}, u32[]{:S(2)}) copy-start(f32[1,12,8,512]{3,2,1,0:T(8,128)S(1)} %collective-permute-done.7.refs_10_.refs_8_) | copy-start | bytes 589828
  39.8 52.8 %collective-permute-start.11 = (f32[3,12,8,512]{3,2,1,0:T(8,128)S(1)}, f32[3,12,8,512]{3,2,1,0:T(8,128)S(1)}, u32[]{:S(2)}, u32[]{:S(2)}) collective-permute-start(f32[3,12,8,512]{3,2,1,0:T(8,128)S(1)} %get-tuple-element.73), channel_id=1, source_target_pairs={{0,8},{4,12},{8,0},{12,4},{1,9},{5,13},{9,1},{13,5},{2,10},{6,14},... | collective-permute-start | bytes 1769480 | tf_op jit(solution)/shard_map/ppermute | solution.py:280
  41.1 6.6 %copy-start.13 = (f32[1,12,8,512]{3,2,1,0:T(8,128)}, f32[1,12,8,512]{3,2,1,0:T(8,128)S(1)}, u32[]{:S(2)}) copy-start(f32[1,12,8,512]{3,2,1,0:T(8,128)S(1)} %collective-permute-done.8.refs_13_.refs_11_) | copy-start | bytes 589828
  41.1 51.5 %collective-permute-start.13 = (f32[3,12,8,512]{3,2,1,0:T(8,128)S(1)}, f32[3,12,8,512]{3,2,1,0:T(8,128)S(1)}, u32[]{:S(2)}, u32[]{:S(2)}) collective-permute-start(f32[3,12,8,512]{3,2,1,0:T(8,128)S(1)} %get-tuple-element.75), channel_id=1, source_target_pairs={{0,12},{4,0},{8,4},{12,8},{1,13},{5,1},{9,5},{13,9},{2,14},{6,2},{... | collective-permute-start | bytes 1769480 | tf_op jit(solution)/shard_map/ppermute | solution.py:280
  47.7 1.4 copy-start.17
  86.3 0.9 copy-start.5
  87.2 0.8 copy-start.6
  88.0 0.7 copy-start.7
  88.7 38.2 %collective-permute-start.10 = (f32[12,4,8,512]{3,2,1,0:T(8,128)S(1)}, f32[12,4,8,512]{3,2,1,0:T(8,128)S(1)}, u32[]{:S(2)}, u32[]{:S(2)}) collective-permute-start(f32[12,4,8,512]{3,2,1,0:T(8,128)S(1)} %get-tuple-element.72), channel_id=1, source_target_pairs={{0,4},{4,8},{8,12},{12,0},{1,5},{5,9},{9,13},{13,1},{2,6},{6,10},{... | collective-permute-start | bytes 2359304 | tf_op jit(solution)/shard_map/ppermute | solution.py:280
  89.0 88.0 %collective-permute-start.12 = (f32[12,4,8,512]{3,2,1,0:T(8,128)}, f32[12,4,8,512]{3,2,1,0:T(8,128)S(1)}, u32[]{:S(2)}, u32[]{:S(2)}) collective-permute-start(f32[12,4,8,512]{3,2,1,0:T(8,128)} %get-tuple-element.74), channel_id=1, source_target_pairs={{0,8},{4,12},{8,0},{12,4},{1,9},{5,13},{9,1},{13,5},{2,10},{6,14},... | collective-permute-start | bytes 2359304 | tf_op jit(solution)/shard_map/ppermute | solution.py:280
  92.5 105.0 %copy-start.8 = (f32[3,12,8,512]{3,2,1,0:T(8,128)}, f32[3,12,8,512]{3,2,1,0:T(8,128)S(1)}, u32[]{:S(2)}) copy-start(f32[3,12,8,512]{3,2,1,0:T(8,128)S(1)} %collective-permute-done.9.refs_8_.refs_6_) | copy-start | bytes 1769476
  92.5 84.5 %collective-permute-start.14 = (f32[12,4,8,512]{3,2,1,0:T(8,128)}, f32[12,4,8,512]{3,2,1,0:T(8,128)S(1)}, u32[]{:S(2)}, u32[]{:S(2)}) collective-permute-start(f32[12,4,8,512]{3,2,1,0:T(8,128)} %get-tuple-element.76), channel_id=1, source_target_pairs={{0,12},{4,0},{8,4},{12,8},{1,13},{5,1},{9,5},{13,9},{2,14},{6,2},{... | collective-permute-start | bytes 2359304 | tf_op jit(solution)/shard_map/ppermute | solution.py:280
  92.6 105.6 %copy-start.9 = (f32[3,12,8,512]{3,2,1,0:T(8,128)}, f32[3,12,8,512]{3,2,1,0:T(8,128)S(1)}, u32[]{:S(2)}) copy-start(f32[3,12,8,512]{3,2,1,0:T(8,128)S(1)} %collective-permute-done.11.refs_11_.refs_9_) | copy-start | bytes 1769476
  92.6 105.6 %copy-start.10 = (f32[3,12,8,512]{3,2,1,0:T(8,128)}, f32[3,12,8,512]{3,2,1,0:T(8,128)S(1)}, u32[]{:S(2)}) copy-start(f32[3,12,8,512]{3,2,1,0:T(8,128)S(1)} %collective-permute-done.13.refs_14_.refs_12_) | copy-start | bytes 1769476
  92.6 104.5 %collective-permute-start.15 = (f32[12,4,8,512]{3,2,1,0:T(8,128)}, f32[12,4,8,512]{3,2,1,0:T(8,128)S(1)}, u32[]{:S(2)}, u32[]{:S(2)}) collective-permute-start(f32[12,4,8,512]{3,2,1,0:T(8,128)} %get-tuple-element.88), channel_id=1, source_target_pairs={{0,4},{4,8},{8,12},{12,0},{1,5},{5,9},{9,13},{13,1},{2,6},{6,10},{... | collective-permute-start | bytes 2359304 | tf_op jit(solution)/shard_map/ppermute | solution.py:280
  126.9 120.4 %collective-permute-start.16 = (f32[12,4,8,512]{3,2,1,0:T(8,128)}, f32[12,4,8,512]{3,2,1,0:T(8,128)}, u32[]{:S(2)}, u32[]{:S(2)}) collective-permute-start(f32[12,4,8,512]{3,2,1,0:T(8,128)} %get-tuple-element.89), channel_id=1, source_target_pairs={{0,8},{4,12},{8,0},{12,4},{1,9},{5,13},{9,1},{13,5},{2,10},{6,14},... | collective-permute-start | bytes 2359304 | tf_op jit(solution)/shard_map/ppermute | solution.py:280
  127.0 71.2 %copy-start.14 = (f32[12,4,8,512]{3,2,1,0:T(8,128)}, f32[12,4,8,512]{3,2,1,0:T(8,128)S(1)}, u32[]{:S(2)}) copy-start(f32[12,4,8,512]{3,2,1,0:T(8,128)S(1)} %collective-permute-done.10.refs_9_.refs_7_) | copy-start | bytes 2359300
  127.0 120.4 %collective-permute-start.17 = (f32[12,4,8,512]{3,2,1,0:T(8,128)}, f32[12,4,8,512]{3,2,1,0:T(8,128)}, u32[]{:S(2)}, u32[]{:S(2)}) collective-permute-start(f32[12,4,8,512]{3,2,1,0:T(8,128)} %get-tuple-element.90), channel_id=1, source_target_pairs={{0,12},{4,0},{8,4},{12,8},{1,13},{5,1},{9,5},{13,9},{2,14},{6,2},{... | collective-permute-start | bytes 2359304 | tf_op jit(solution)/shard_map/ppermute | solution.py:280
  177.0 21.2 %copy-start.15 = (f32[12,4,8,512]{3,2,1,0:T(8,128)}, f32[12,4,8,512]{3,2,1,0:T(8,128)S(1)}, u32[]{:S(2)}) copy-start(f32[12,4,8,512]{3,2,1,0:T(8,128)S(1)} %collective-permute-done.12.refs_12_.refs_10_) | copy-start | bytes 2359300
  177.0 21.2 %copy-start.16 = (f32[12,4,8,512]{3,2,1,0:T(8,128)}, f32[12,4,8,512]{3,2,1,0:T(8,128)S(1)}, u32[]{:S(2)}) copy-start(f32[12,4,8,512]{3,2,1,0:T(8,128)S(1)} %collective-permute-done.14.refs_15_.refs_13_) | copy-start | bytes 2359300
  177.0 112.9 %collective-permute-start.21 = (f32[12,3,8,512]{3,2,1,0:T(8,128)S(1)}, f32[12,3,8,512]{3,2,1,0:T(8,128)S(1)}, u32[]{:S(2)}, u32[]{:S(2)}) collective-permute-start(f32[12,3,8,512]{3,2,1,0:T(8,128)S(1)} %get-tuple-element.100), channel_id=1, source_target_pairs={{0,4},{4,8},{8,12},{12,0},{1,5},{5,9},{9,13},{13,1},{2,6},{6,10},{... | collective-permute-start | bytes 1769480 | tf_op jit(solution)/shard_map/ppermute | solution.py:280
  195.2 110.1 %collective-permute-start.22 = (f32[12,3,8,512]{3,2,1,0:T(8,128)S(1)}, f32[12,3,8,512]{3,2,1,0:T(8,128)}, u32[]{:S(2)}, u32[]{:S(2)}) collective-permute-start(f32[12,3,8,512]{3,2,1,0:T(8,128)S(1)} %get-tuple-element.101), channel_id=1, source_target_pairs={{0,8},{4,12},{8,0},{12,4},{1,9},{5,13},{9,1},{13,5},{2,10},{6,14},... | collective-permute-start | bytes 1769480 | tf_op jit(solution)/shard_map/ppermute | solution.py:280
  197.1 1.1 copy-start.18
  197.1 108.2 %collective-permute-start.23 = (f32[12,3,8,512]{3,2,1,0:T(8,128)S(1)}, f32[12,3,8,512]{3,2,1,0:T(8,128)}, u32[]{:S(2)}, u32[]{:S(2)}) collective-permute-start(f32[12,3,8,512]{3,2,1,0:T(8,128)S(1)} %get-tuple-element.102), channel_id=1, source_target_pairs={{0,12},{4,0},{8,4},{12,8},{1,13},{5,1},{9,5},{13,9},{2,14},{6,2},{... | collective-permute-start | bytes 1769480 | tf_op jit(solution)/shard_map/ppermute | solution.py:280
  247.4 64.4 %collective-permute-start.18 = (f32[12,1,8,512]{3,2,1,0:T(8,128)S(1)}, f32[12,1,8,512]{3,2,1,0:T(8,128)S(1)}, u32[]{:S(2)}, u32[]{:S(2)}) collective-permute-start(f32[12,1,8,512]{3,2,1,0:T(8,128)S(1)} %get-tuple-element.92), channel_id=1, source_target_pairs={{0,4},{4,8},{8,12},{12,0},{1,5},{5,9},{9,13},{13,1},{2,6},{6,10},{... | collective-permute-start | bytes 589832 | tf_op jit(solution)/shard_map/ppermute | solution.py:280
  286.2 25.6 %collective-permute-start.19 = (f32[12,1,8,512]{3,2,1,0:T(8,128)S(1)}, f32[12,1,8,512]{3,2,1,0:T(8,128)S(1)}, u32[]{:S(2)}, u32[]{:S(2)}) collective-permute-start(f32[12,1,8,512]{3,2,1,0:T(8,128)S(1)} %get-tuple-element.93), channel_id=1, source_target_pairs={{0,8},{4,12},{8,0},{12,4},{1,9},{5,13},{9,1},{13,5},{2,10},{6,14},... | collective-permute-start | bytes 589832 | tf_op jit(solution)/shard_map/ppermute | solution.py:280
  289.9 15.4 %copy-start.19 = (f32[12,3,8,512]{3,2,1,0:T(8,128)}, f32[12,3,8,512]{3,2,1,0:T(8,128)S(1)}, u32[]{:S(2)}) copy-start(f32[12,3,8,512]{3,2,1,0:T(8,128)S(1)} %collective-permute-done.21.refs_7_) | copy-start | bytes 1769476
  289.9 21.9 %collective-permute-start.20 = (f32[12,1,8,512]{3,2,1,0:T(8,128)S(1)}, f32[12,1,8,512]{3,2,1,0:T(8,128)S(1)}, u32[]{:S(2)}, u32[]{:S(2)}) collective-permute-start(f32[12,1,8,512]{3,2,1,0:T(8,128)S(1)} %get-tuple-element.94), channel_id=1, source_target_pairs={{0,12},{4,0},{8,4},{12,8},{1,13},{5,1},{9,5},{13,9},{2,14},{6,2},{... | collective-permute-start | bytes 589832 | tf_op jit(solution)/shard_map/ppermute | solution.py:280
  311.8 0.7 copy-start.20
  311.8 0.7 copy-start.21
  312.5 0.7 copy-start.22

commit v3 on v2

--- a/solution.py
+++ b/solution.py
@@ -129,7 +129,7 @@
         cost_estimate=cost(3),
         name="edges",
     )(*[ensemble] * 8, *statics, *after)
-    return halo(packed)
+    return packed
 
 
 def halo(packed):
@@ -460,17 +460,20 @@
         got = exchange(pieces)
         return [x.reshape(x.shape[0], x.shape[1], PAD, width) for x in got]
 
-    halo_early = edges(ensemble, 0, early, fields, ())
-    groups, starts = [], []
+    packed_early = edges(ensemble, 0, early, fields, ())
+    packed_late = edges(ensemble, early, held - early, (), (packed_early[0],))
+    halo_early = halo(packed_early)
+    groups = []
     for start, stop in [(0, first)] + ([(first, early)] if early > first else []):
         (sent,) = forecast(ensemble, start, stop - start, fields, halo_early, start, halo_early, early, size, [(0, total)])
         groups.append(sent)
-    halo_late = edges(ensemble, early, held - early, (), (groups[0][0],))
-    whole = [received(sent) for sent in groups]
-    halo_late = tied(halo_late, whole[0])
+    whole = [received(groups[0])]
+    whole += [received(sent) for sent in groups[1:]]
+    halo_late = tied(halo(tied(packed_late, halo_early)), whole[0])
     sent_late = forecast(ensemble, early, held - early, fields, halo_late, 0, halo_early, early, size, ranges)
-    late = [received(sent_late[0]), received(tied(sent_late[1], whole[-1]))]
-    late.append(received(tied(sent_late[2], late[0])))
+    late = [received(sent_late[0])]
+    late.append(received(tied(sent_late[1], whole[-1])))
+    late += [received(tied(x, late[0])) for x in sent_late[2:-1]]
 
     def woven(pieces, offset):
         return [x for per_source in zip(*whole, pieces) for x in per_source], ([offset] * len(whole) + [0]) * parts
@@ -479,10 +482,11 @@
     packed = observe(heights, per_field, members, obs_cell, obs_count, obs_value, obs_error)
     packed = lax.psum(packed, ("blk", "sub"))
     mixers = transform(packed, members)
-    late += [received(tied(x, late[1], mixers)) for x in sent_late[3:]]
     shape = (members, total, PAD, width)
-    out = None
-    for (start, stop), pieces in zip(ranges, late):
+    out = analyse(mixers, *woven(late[0], 0), *ranges[0], shape, None)
+    last, out = lax.optimization_barrier((tied(sent_late[-1], late[1]), out))
+    late.append(received(last))
+    for (start, stop), pieces in list(zip(ranges, late))[1:]:
         out = analyse(mixers, *woven(pieces, start), start, stop, shape, out)
     return out.reshape(members, 3, 1, lines, columns)
 

time: 317 us -> 330 us (1.041)
  waiting for transfers between devices: 55.1 us -> 89.1 us
  starting transfers between devices: 120 us -> 98.3 us
    ppermute x18, waiting for transfers between devices: 47.8 us -> 86.3 us  [exchange(): lax.ppermute(pieces[shift], 'grid', [(i, (i + shift) % parts) for i in ra...]
    ppermute x18, starting transfers between devices: 115 us -> 93.3 us  [exchange(): lax.ppermute(pieces[shift], 'grid', [(i, (i + shift) % parts) for i in ra...]
    ppermute x2, waiting for transfers between devices: 4.53 us -> 0.01 us  [halo(): lax.ppermute(packed[1], ('blk', 'sub'), [(0, 3), (3, 0), (1, 2), (2, 1)])]
    unnamed x48 -> x54, local copies, waits for them, and re-layouts: 6.76 us -> 7.83 us
  transfers between devices with their start and end apart: 24 -> 24, of which waited for: 3 -> 3; matrix products, arithmetic and copies ran while one was open for 0% -> 0% of each run, Pallas kernels for 27% -> 29%
where the time goes in v3:
time: 330 us; the launch traced here: 328 us
  Pallas kernels  102 us (31%)
  starting transfers between devices  98.3 us (30%)
  waiting for transfers between devices  89.1 us (27%)
  blocking collectives  30.2 us (9%)
  local copies, waits for them, and re-layouts  7.83 us (2%)
    ppermute x18, starting transfers between devices, exchange(): lax.ppermute(pieces[shift], 'grid', [(i, (i + shift) % parts) for i in ra...  93.3 us
    ppermute x18, waiting for transfers between devices, exchange(): lax.ppermute(pieces[shift], 'grid', [(i, (i + shift) % parts) for i in ra...  86.3 us
    pallas_call x3, Pallas kernels, forecast(): pl.pallas_call(functools.partial(forecast_kernel, parts=parts, tiles=tile...  51.2 us
    psum x1, blocking collectives, shards(): packed = lax.psum(packed, ('blk', 'sub'))  30.2 us
    pallas_call x4, Pallas kernels, analyse(): pl.pallas_call(functools.partial(analysis_kernel, carried=int(carried is...  25.1 us
    pallas_call x1, Pallas kernels, transform(): pl.pallas_call(functools.partial(transform_kernel, parts=parts, members=m...  12.2 us
    pallas_call x2, Pallas kernels, edges(): pl.pallas_call(functools.partial(pack_kernel, chunk=chunk, two=two, stati...  7.97 us
    unnamed x54, local copies, waits for them, and re-layouts  7.83 us
  transfers between devices with their start and end apart: 24, of which 3 were waited for; matrix products, arithmetic and copies ran while one was open for 0% of the time, Pallas kernels for 29%

profile of v3, /device:TPU:0, one launch (start us, length us, event | category | flops | bytes accessed | tf_op | source)
XLA Modules:
  0.0 328.4 jit_solution(2376212825536296658)
XLA Ops:
  0.0 2.9 edges.2
  2.9 0.5 collective-permute-start.1
  3.4 2.5 collective-permute-start
  5.9 0.1 collective-permute-start.2
  6.0 5.1 %edges.3 = (f32[12,3,4,512]{3,2,1,0:T(4,128)}, f32[12,3,4,128]{3,2,1,0:T(4,128)}, f32[12,3,128,128]{3,2,1,0:T(8,128)}) custom-call(f32[16,3,128,512]{3,2,1,0:T(8,128)} %refs_0_.9, f32[16,3,128,512]{3,2,1,0:T(8,128)} %refs_0_.9, f32[16,3,128,512]{3,2,1,0:T(8,128)} %refs_0_.9, f32[16,3,128,512]{3,2,1,0:T(8,128)} %refs_0_.9, f32[16,3,128,512]{3,2,1,0:T(8,128)} %refs_0_.9, ...), custom_call_target="tpu_custom_call" | custom-call | flops 3000000 | bytes 9000 | tf_op jit(solution)/shard_map/edges/pallas_call | solution.py:123
  11.1 0.0 collective-permute-done.2.refs_6_.refs_7_.refs_11_.refs_12_
  11.1 0.0 collective-permute-done.1.refs_5_.refs_10_
  11.1 0.3 collective-permute-start.4
  11.4 4.1 %forecast.3 = (f32[1,12,8,512]{3,2,1,0:T(8,128)S(1)}, f32[1,12,8,512]{3,2,1,0:T(8,128)S(1)}, f32[1,12,8,512]{3,2,1,0:T(8,128)S(1)}, f32[1,12,8,512]{3,2,1,0:T(8,128)S(1)}) custom-call(f32[16,3,128,512]{3,2,1,0:T(8,128)} %refs_0_.9, f32[128,512]{1,0:T(8,128)S(1)} %copy-done.3, s32[128,512]{1,0:T(8,128)S(1)} %copy-done.4, ...), custom_call_target="tpu_custom_call" | custom-call | flops 3000000 | bytes 9000 | tf_op jit(solution)/shard_map/forecast/pallas_call | solution.py:262
  15.5 0.7 copy-done.2
  16.2 1.8 collective-permute-start.6
  18.0 1.1 collective-permute-start.5
  19.1 2.6 collective-permute-start.7
  21.7 1.3 collective-permute-start.8
  23.0 10.0 %forecast.4 = (f32[3,12,8,512]{3,2,1,0:T(8,128)S(1)}, f32[3,12,8,512]{3,2,1,0:T(8,128)S(1)}, f32[3,12,8,512]{3,2,1,0:T(8,128)S(1)}, f32[3,12,8,512]{3,2,1,0:T(8,128)S(1)}) custom-call(f32[16,3,128,512]{3,2,1,0:T(8,128)} %refs_0_.9, f32[128,512]{1,0:T(8,128)S(1)} %copy-done.3, s32[128,512]{1,0:T(8,128)S(1)} %copy-done.4, ...), custom_call_target="tpu_custom_call" | custom-call | flops 9000000 | bytes 27000 | tf_op jit(solution)/shard_map/forecast/pallas_call | solution.py:262
  33.0 0.8 copy-done.1
  33.8 0.0 collective-permute-done.5.refs_6_.refs_7_
  33.8 0.7 collective-permute-start.9
  34.5 0.6 collective-permute-start.3
  35.1 0.0 collective-permute-done.7.refs_10_.refs_8_
  35.1 1.5 collective-permute-start.11
  36.6 0.0 collective-permute-done.8.refs_13_.refs_11_
  36.6 3.7 %collective-permute-start.13 = (f32[3,12,8,512]{3,2,1,0:T(8,128)S(1)}, f32[3,12,8,512]{3,2,1,0:T(8,128)S(1)}, u32[]{:S(2)}, u32[]{:S(2)}) collective-permute-start(f32[3,12,8,512]{3,2,1,0:T(8,128)S(1)} %get-tuple-element.86), channel_id=1, source_target_pairs={{0,12},{4,0},{8,4},{12,8},{1,13},{5,1},{9,5},{13,9},{2,14},{6,2},{... | collective-permute-start | bytes 1769480 | tf_op jit(solution)/shard_map/ppermute | solution.py:280
  40.4 2.8 collective-permute-done.3.refs_3_.refs_4_
  43.1 0.0 collective-permute-done.4.refs_5_
  43.1 1.4 copy-done.17
  44.5 37.2 %forecast.5 = (f32[12,4,8,512]{3,2,1,0:T(8,128)S(1)}, f32[12,4,8,512]{3,2,1,0:T(8,128)S(1)}, f32[12,4,8,512]{3,2,1,0:T(8,128)}, f32[12,4,8,512]{3,2,1,0:T(8,128)...) custom-call(f32[16,3,128,512]{3,2,1,0:T(8,128)} %refs_0_.9, ...), custom_call_target="tpu_custom_call" | custom-call | flops 36000000 | bytes 108000 | tf_op jit(solution)/shard_map/forecast/pallas_call | solution.py:262
  81.8 0.9 copy-done.5
  82.6 0.8 copy-done.6
  83.5 0.7 copy-done.7
  84.1 0.3 collective-permute-start.10
  84.5 3.5 %collective-permute-start.12 = (f32[12,4,8,512]{3,2,1,0:T(8,128)}, f32[12,4,8,512]{3,2,1,0:T(8,128)S(1)}, u32[]{:S(2)}, u32[]{:S(2)}) collective-permute-start(f32[12,4,8,512]{3,2,1,0:T(8,128)} %get-tuple-element.85), channel_id=1, source_target_pairs={{0,8},{4,12},{8,0},{12,4},{1,9},{5,13},{9,1},{13,5},{2,10},{6,14},... | collective-permute-start | bytes 2359304 | tf_op jit(solution)/shard_map/ppermute | solution.py:280
  88.0 0.1 collective-permute-start.14
  88.0 0.0 collective-permute-done.13.refs_14_.refs_12_
  88.0 34.3 %collective-permute-start.15 = (f32[12,4,8,512]{3,2,1,0:T(8,128)}, f32[12,4,8,512]{3,2,1,0:T(8,128)S(1)}, u32[]{:S(2)}, u32[]{:S(2)}) collective-permute-start(f32[12,4,8,512]{3,2,1,0:T(8,128)} %get-tuple-element.99), channel_id=1, source_target_pairs={{0,4},{4,8},{8,12},{12,0},{1,5},{5,9},{9,13},{13,1},{2,6},{6,10},{... | collective-permute-start | bytes 2359304 | tf_op jit(solution)/shard_map/ppermute | solution.py:280
  122.3 0.0 collective-permute-start.16
  122.3 0.0 collective-permute-done.10.refs_9_.refs_7_
  122.3 2.4 collective-permute-start.17
  124.7 47.7 %collective-permute-done.12.refs_12_.refs_10_ = f32[12,4,8,512]{3,2,1,0:T(8,128)S(1)} collective-permute-done((f32[12,4,8,512]{3,2,1,0:T(8,128)}, f32[12,4,8,512]{3,2,1,0:T(8,128)S(1)}, u32[]{:S(2)}, u32[]{:S(2)}) %collective-permute-start.12) | collective-permute-done | bytes 786464 | tf_op jit(solution)/shard_map/ppermute | solution.py:280
  172.4 0.0 collective-permute-done.14.refs_15_.refs_13_
  172.4 18.1 %collective-permute-start.21 = (f32[12,3,8,512]{3,2,1,0:T(8,128)S(1)}, f32[12,3,8,512]{3,2,1,0:T(8,128)S(1)}, u32[]{:S(2)}, u32[]{:S(2)}) collective-permute-start(f32[12,3,8,512]{3,2,1,0:T(8,128)S(1)} %get-tuple-element.115), channel_id=1, source_target_pairs={{0,4},{4,8},{8,12},{12,0},{1,5},{5,9},{9,13},{13,1},{2,6},{6,10},{... | collective-permute-start | bytes 1769480 | tf_op jit(solution)/shard_map/ppermute | solution.py:280
  190.6 2.0 collective-permute-start.22
  192.6 0.0 collective-permute-done.15.refs_7_
  192.6 0.3 collective-permute-start.23
  193.6 38.5 %collective-permute-done.16.refs_10_ = f32[12,4,8,512]{3,2,1,0:T(8,128)S(1)} collective-permute-done((f32[12,4,8,512]{3,2,1,0:T(8,128)}, f32[12,4,8,512]{3,2,1,0:T(8,128)S(1)}, u32[]{:S(2)}, u32[]{:S(2)}) %collective-permute-start.16) | collective-permute-done | bytes 786464 | tf_op jit(solution)/shard_map/ppermute | solution.py:280
  232.1 0.0 collective-permute-done.17.refs_13_
  232.2 0.8 copy-done.19
  233.0 0.2 copy-done.20
  233.3 5.5 %observe.1 = f32[72,64]{1,0:T(8,128)} custom-call(s32[1,1]{1,0:T(1,128)} %bitcast.7.refs_0_, s32[1,64]{1,0:T(1,128)} %bitcast.8, f32[1,64]{1,0:T(1,128)} %bitcast.9, f32[1,64]{1,0:T(1,128)} %bitcast.10, f32[1,12,8,512]{3,2,1,0:T(8,128)} %copy-done.2, f32[3,12,8,512]{3,2,1,0:T(8,128)} %copy-done.1, f32[12,4,8,512]{3,2,1,0:T(8,128)} %copy-done.5, ...), custom_call_target="tpu_custom_call" | custom-call | flops 6000000 | bytes 18000 | tf_op jit(solution)/shard_map/observe/pallas_call | solution.py:336
  238.8 30.2 %psum.7.packed = f32[72,64]{1,0:T(8,128)} all-reduce(f32[72,64]{1,0:T(8,128)} %observe.1), channel_id=1, replica_groups=mesh['copy'=2,'grid'=4,'blk'=2,'sub'=2] {'blk','sub'}, use_global_device_ids=true, to_apply=%region_0.0 | all-reduce | flops 4608 | bytes 36864 | tf_op jit(solution)/shard_map/psum | solution.py:483
  269.0 12.2 %transform.1 = (bf16[512,512]{1,0:T(8,128)(2,1)}, bf16[512,512]{1,0:T(8,128)(2,1)}) custom-call(f32[72,64]{1,0:T(8,128)} %psum.7.packed), custom_call_target="tpu_custom_call" | custom-call | flops 12000000 | bytes 36000 | tf_op jit(solution)/shard_map/transform/pallas_call | solution.py:405
  281.2 7.5 %analysis.4.refs_14_ = f32[64,12,8,512]{3,2,1,0:T(8,128)} custom-call(bf16[512,512]{1,0:T(8,128)(2,1)} %get-tuple-element.88.refs_0_, bf16[512,512]{1,0:T(8,128)(2,1)} %get-tuple-element.89.refs_1_, f32[1,12,8,512]{3,2,1,0:T(8,128)} %copy-done.2, f32[3,12,8,512]{3,2,1,0:T(8,128)} %copy-done.1, f32[12,4,8,512]{3,2,1,0:T(8,128)} %copy-done.5, ...), custom_call_target="tpu_custom_call" | custom-call | flops 8000000 | bytes 24000 | tf_op jit(solution)/shard_map/analysis/pallas_call | solution.py:433
  288.7 17.3 %collective-permute-start.18 = (f32[12,1,8,512]{3,2,1,0:T(8,128)S(1)}, f32[12,1,8,512]{3,2,1,0:T(8,128)S(1)}, u32[]{:S(2)}, u32[]{:S(2)}) collective-permute-start(f32[12,1,8,512]{3,2,1,0:T(8,128)S(1)} %get-tuple-element.107), channel_id=1, source_target_pairs={{0,4},{4,8},{8,12},{12,0},{1,5},{5,9},{9,13},{13,1},{2,6},{6,10},{... | collective-permute-start | bytes 589832 | tf_op jit(solution)/shard_map/ppermute | solution.py:280
  306.0 3.3 collective-permute-start.19
  309.3 0.0 collective-permute-done.21.refs_7_
  309.3 0.0 collective-permute-start.20
  309.3 7.7 %analysis.5.refs_14_ = f32[64,12,8,512]{3,2,1,0:T(8,128)} custom-call(bf16[512,512]{1,0:T(8,128)(2,1)} %get-tuple-element.88.refs_0_, bf16[512,512]{1,0:T(8,128)(2,1)} %get-tuple-element.89.refs_1_, f32[1,12,8,512]{3,2,1,0:T(8,128)} %copy-done.2, f32[3,12,8,512]{3,2,1,0:T(8,128)} %copy-done.1, ...), custom_call_target="tpu_custom_call", output_to_operand_aliasing={{}: (14, {})} | custom-call | flops 8000000 | bytes 24000 | tf_op jit(solution)/shard_map/analysis/pallas_call | solution.py:433
  317.0 0.0 collective-permute-done.22.refs_10_
  317.0 6.5 %analysis.6.refs_14_ = f32[64,12,8,512]{3,2,1,0:T(8,128)} custom-call(bf16[512,512]{1,0:T(8,128)(2,1)} %get-tuple-element.88.refs_0_, bf16[512,512]{1,0:T(8,128)(2,1)} %get-tuple-element.89.refs_1_, f32[1,12,8,512]{3,2,1,0:T(8,128)} %copy-done.2, f32[3,12,8,512]{3,2,1,0:T(8,128)} %copy-done.1, ...), custom_call_target="tpu_custom_call", output_to_operand_aliasing={{}: (14, {})} | custom-call | flops 6000000 | bytes 18000 | tf_op jit(solution)/shard_map/analysis/pallas_call | solution.py:433
  323.5 0.0 collective-permute-done.19.refs_10_
  323.5 0.6 copy-done.22
  324.2 0.1 copy-done.23
  324.2 0.7 copy-done.24
  324.9 3.5 %analysis.7 = f32[64,12,8,512]{3,2,1,0:T(8,128)} custom-call(bf16[512,512]{1,0:T(8,128)(2,1)} %get-tuple-element.88.refs_0_, bf16[512,512]{1,0:T(8,128)(2,1)} %get-tuple-element.89.refs_1_, f32[1,12,8,512]{3,2,1,0:T(8,128)} %copy-done.2, f32[3,12,8,512]{3,2,1,0:T(8,128)} %copy-done.1, f32[12,1,8,512]{3,2,1,0:T(8,128)} %copy-done.7, ...), custom_call_target="tpu_custom_call", output_to_operand_aliasing={{}: (14, {})} | custom-call | flops 2000000 | bytes 6000 | tf_op jit(solution)/shard_map/analysis/pallas_call | solution.py:433
  (50 shorter events, 0.1 us)
Async XLA Ops:
  2.9 8.2 %collective-permute-start.1 = (f32[5,3,128,128]{3,2,1,0:T(8,128)}, f32[5,3,128,128]{3,2,1,0:T(8,128)S(1)}, u32[]{:S(2)}, u32[]{:S(2)}) collective-permute-start(f32[5,3,128,128]{3,2,1,0:T(8,128)} %get-tuple-element.63), channel_id=1, source_target_pairs={{0,1},{1,0},{2,3},{3,2},{4,5},{5,4},{6,7},{7,6},{8,9},{9,8},{10,11... | collective-permute-start | bytes 2949128 | tf_op jit(solution)/shard_map/ppermute | solution.py:137
  3.4 7.7 %collective-permute-start = (f32[5,3,4,512]{3,2,1,0:T(4,128)}, f32[5,3,4,512]{3,2,1,0:T(4,128)S(1)}, u32[]{:S(2)}, u32[]{:S(2)}) collective-permute-start(f32[5,3,4,512]{3,2,1,0:T(4,128)} %get-tuple-element.62.refs_8_), channel_id=1, source_target_pairs={{0,2},{2,0},{1,3},{3,1},{4,6},{6,4},{5,7},{7,5},{8,10},{10,8},{9,1... | collective-permute-start | bytes 368648 | tf_op jit(solution)/shard_map/ppermute | solution.py:139
  5.8 5.5 %copy-start.3 = (f32[128,512]{1,0:T(8,128)S(1)}, f32[128,512]{1,0:T(8,128)}, u32[]{:S(2)}) copy-start(f32[128,512]{1,0:T(8,128)} %refs_1_.9) | copy-start | bytes 786436
  5.8 5.5 %copy-start.4 = (s32[128,512]{1,0:T(8,128)S(1)}, s32[128,512]{1,0:T(8,128)}, u32[]{:S(2)}) copy-start(s32[128,512]{1,0:T(8,128)} %refs_2_.9) | copy-start | bytes 786436
  5.9 5.2 %collective-permute-start.2 = (f32[5,3,4,128]{3,2,1,0:T(4,128)}, f32[5,3,4,128]{3,2,1,0:T(4,128)S(1)}, u32[]{:S(2)}, u32[]{:S(2)}) collective-permute-start(f32[5,3,4,128]{3,2,1,0:T(4,128)} %get-tuple-element.64), channel_id=1, source_target_pairs={{0,3},{3,0},{1,2},{2,1},{4,7},{7,4},{5,6},{6,5},{8,11},{11,8},{9,1... | collective-permute-start | bytes 92168 | tf_op jit(solution)/shard_map/ppermute | solution.py:140
  11.1 6.9 %copy-start.26 = (f32[12,3,4,128]{3,2,1,0:T(4,128)S(1)}, f32[12,3,4,128]{3,2,1,0:T(4,128)}, u32[]{:S(2)}) copy-start(f32[12,3,4,128]{3,2,1,0:T(4,128)} %get-tuple-element.72) | copy-start | bytes 221188
  11.1 21.9 %copy-start = (f32[5,3,128,128]{3,2,1,0:T(8,128)}, f32[5,3,128,128]{3,2,1,0:T(8,128)S(1)}, u32[]{:S(2)}) copy-start(f32[5,3,128,128]{3,2,1,0:T(8,128)S(1)} %collective-permute-done.1.refs_5_.refs_10_) | copy-start | bytes 2949124
  11.1 23.4 %copy-start.25 = (f32[12,3,4,512]{3,2,1,0:T(4,128)S(1)}, f32[12,3,4,512]{3,2,1,0:T(4,128)}, u32[]{:S(2)}) copy-start(f32[12,3,4,512]{3,2,1,0:T(4,128)} %get-tuple-element.70) | copy-start | bytes 884740
  11.1 32.0 %collective-permute-start.4 = (f32[12,3,128,128]{3,2,1,0:T(8,128)}, f32[12,3,128,128]{3,2,1,0:T(8,128)S(1)}, u32[]{:S(2)}, u32[]{:S(2)}) collective-permute-start(f32[12,3,128,128]{3,2,1,0:T(8,128)} %get-tuple-element.71), channel_id=1, source_target_pairs={{0,1},{1,0},{2,3},{3,2},{4,5},{5,4},{6,7},{7,6},{8,9},{9,8},{10,11... | collective-permute-start | bytes 7077896 | tf_op jit(solution)/shard_map/ppermute | solution.py:137
  15.5 0.7 copy-start.2
  16.2 18.3 %collective-permute-start.6 = (f32[1,12,8,512]{3,2,1,0:T(8,128)S(1)}, f32[1,12,8,512]{3,2,1,0:T(8,128)S(1)}, u32[]{:S(2)}, u32[]{:S(2)}) collective-permute-start(f32[1,12,8,512]{3,2,1,0:T(8,128)S(1)} %get-tuple-element.73), channel_id=1, source_target_pairs={{0,4},{4,8},{8,12},{12,0},{1,5},{5,9},{9,13},{13,1},{2,6},{6,10},{... | collective-permute-start | bytes 589832 | tf_op jit(solution)/shard_map/ppermute | solution.py:280
  18.0 15.8 %collective-permute-start.5 = (f32[12,3,4,128]{3,2,1,0:T(4,128)S(1)}, f32[12,3,4,128]{3,2,1,0:T(4,128)S(1)}, u32[]{:S(2)}, u32[]{:S(2)}) collective-permute-start(f32[12,3,4,128]{3,2,1,0:T(4,128)S(1)} %copy-done.26), channel_id=1, source_target_pairs={{0,3},{3,0},{1,2},{2,1},{4,7},{7,4},{5,6},{6,5},{8,11},{11,8},{9,1... | collective-permute-start | bytes 221192 | tf_op jit(solution)/shard_map/ppermute | solution.py:140
  19.1 16.0 %collective-permute-start.7 = (f32[1,12,8,512]{3,2,1,0:T(8,128)S(1)}, f32[1,12,8,512]{3,2,1,0:T(8,128)S(1)}, u32[]{:S(2)}, u32[]{:S(2)}) collective-permute-start(f32[1,12,8,512]{3,2,1,0:T(8,128)S(1)} %get-tuple-element.74), channel_id=1, source_target_pairs={{0,8},{4,12},{8,0},{12,4},{1,9},{5,13},{9,1},{13,5},{2,10},{6,14},... | collective-permute-start | bytes 589832 | tf_op jit(solution)/shard_map/ppermute | solution.py:280
  21.7 15.0 %collective-permute-start.8 = (f32[1,12,8,512]{3,2,1,0:T(8,128)S(1)}, f32[1,12,8,512]{3,2,1,0:T(8,128)S(1)}, u32[]{:S(2)}, u32[]{:S(2)}) collective-permute-start(f32[1,12,8,512]{3,2,1,0:T(8,128)S(1)} %get-tuple-element.75), channel_id=1, source_target_pairs={{0,12},{4,0},{8,4},{12,8},{1,13},{5,1},{9,5},{13,9},{2,14},{6,2},{... | collective-permute-start | bytes 589832 | tf_op jit(solution)/shard_map/ppermute | solution.py:280
  33.0 0.8 copy-start.1
  33.8 54.2 %collective-permute-start.9 = (f32[3,12,8,512]{3,2,1,0:T(8,128)S(1)}, f32[3,12,8,512]{3,2,1,0:T(8,128)S(1)}, u32[]{:S(2)}, u32[]{:S(2)}) collective-permute-start(f32[3,12,8,512]{3,2,1,0:T(8,128)S(1)} %get-tuple-element.82), channel_id=1, source_target_pairs={{0,4},{4,8},{8,12},{12,0},{1,5},{5,9},{9,13},{13,1},{2,6},{6,10},{... | collective-permute-start | bytes 1769480 | tf_op jit(solution)/shard_map/ppermute | solution.py:280
  34.5 198.8 %copy-start.11 = (f32[1,12,8,512]{3,2,1,0:T(8,128)}, f32[1,12,8,512]{3,2,1,0:T(8,128)S(1)}, u32[]{:S(2)}) copy-start(f32[1,12,8,512]{3,2,1,0:T(8,128)S(1)} %collective-permute-done.6.refs_7_.refs_5_) | copy-start | bytes 589828
  34.5 8.6 %collective-permute-start.3 = (f32[12,3,4,512]{3,2,1,0:T(4,128)S(1)}, f32[12,3,4,512]{3,2,1,0:T(4,128)S(1)}, u32[]{:S(2)}, u32[]{:S(2)}) collective-permute-start(f32[12,3,4,512]{3,2,1,0:T(4,128)S(1)} %copy-done.25), channel_id=1, source_target_pairs={{0,2},{2,0},{1,3},{3,1},{4,6},{6,4},{5,7},{7,5},{8,10},{10,8},{9,1... | collective-permute-start | bytes 884744 | tf_op jit(solution)/shard_map/ppermute | solution.py:139
  35.1 198.2 %copy-start.12 = (f32[1,12,8,512]{3,2,1,0:T(8,128)}, f32[1,12,8,512]{3,2,1,0:T(8,128)S(1)}, u32[]{:S(2)}) copy-start(f32[1,12,8,512]{3,2,1,0:T(8,128)S(1)} %collective-permute-done.7.refs_10_.refs_8_) | copy-start | bytes 589828
  35.1 52.9 %collective-permute-start.11 = (f32[3,12,8,512]{3,2,1,0:T(8,128)S(1)}, f32[3,12,8,512]{3,2,1,0:T(8,128)S(1)}, u32[]{:S(2)}, u32[]{:S(2)}) collective-permute-start(f32[3,12,8,512]{3,2,1,0:T(8,128)S(1)} %get-tuple-element.84), channel_id=1, source_target_pairs={{0,8},{4,12},{8,0},{12,4},{1,9},{5,13},{9,1},{13,5},{2,10},{6,14},... | collective-permute-start | bytes 1769480 | tf_op jit(solution)/shard_map/ppermute | solution.py:280
  36.6 6.5 %copy-start.13 = (f32[1,12,8,512]{3,2,1,0:T(8,128)}, f32[1,12,8,512]{3,2,1,0:T(8,128)S(1)}, u32[]{:S(2)}) copy-start(f32[1,12,8,512]{3,2,1,0:T(8,128)S(1)} %collective-permute-done.8.refs_13_.refs_11_) | copy-start | bytes 589828
  36.6 51.4 %collective-permute-start.13 = (f32[3,12,8,512]{3,2,1,0:T(8,128)S(1)}, f32[3,12,8,512]{3,2,1,0:T(8,128)S(1)}, u32[]{:S(2)}, u32[]{:S(2)}) collective-permute-start(f32[3,12,8,512]{3,2,1,0:T(8,128)S(1)} %get-tuple-element.86), channel_id=1, source_target_pairs={{0,12},{4,0},{8,4},{12,8},{1,13},{5,1},{9,5},{13,9},{2,14},{6,2},{... | collective-permute-start | bytes 1769480 | tf_op jit(solution)/shard_map/ppermute | solution.py:280
  43.1 1.4 copy-start.17
  81.7 0.9 copy-start.5
  82.6 0.8 copy-start.6
  83.5 0.7 copy-start.7
  84.1 38.2 %collective-permute-start.10 = (f32[12,4,8,512]{3,2,1,0:T(8,128)S(1)}, f32[12,4,8,512]{3,2,1,0:T(8,128)S(1)}, u32[]{:S(2)}, u32[]{:S(2)}) collective-permute-start(f32[12,4,8,512]{3,2,1,0:T(8,128)S(1)} %get-tuple-element.83), channel_id=1, source_target_pairs={{0,4},{4,8},{8,12},{12,0},{1,5},{5,9},{9,13},{13,1},{2,6},{6,10},{... | collective-permute-start | bytes 2359304 | tf_op jit(solution)/shard_map/ppermute | solution.py:280
  84.5 87.9 %collective-permute-start.12 = (f32[12,4,8,512]{3,2,1,0:T(8,128)}, f32[12,4,8,512]{3,2,1,0:T(8,128)S(1)}, u32[]{:S(2)}, u32[]{:S(2)}) collective-permute-start(f32[12,4,8,512]{3,2,1,0:T(8,128)} %get-tuple-element.85), channel_id=1, source_target_pairs={{0,8},{4,12},{8,0},{12,4},{1,9},{5,13},{9,1},{13,5},{2,10},{6,14},... | collective-permute-start | bytes 2359304 | tf_op jit(solution)/shard_map/ppermute | solution.py:280
  88.0 105.0 %copy-start.8 = (f32[3,12,8,512]{3,2,1,0:T(8,128)}, f32[3,12,8,512]{3,2,1,0:T(8,128)S(1)}, u32[]{:S(2)}) copy-start(f32[3,12,8,512]{3,2,1,0:T(8,128)S(1)} %collective-permute-done.9.refs_8_.refs_6_) | copy-start | bytes 1769476
  88.0 84.4 %collective-permute-start.14 = (f32[12,4,8,512]{3,2,1,0:T(8,128)}, f32[12,4,8,512]{3,2,1,0:T(8,128)S(1)}, u32[]{:S(2)}, u32[]{:S(2)}) collective-permute-start(f32[12,4,8,512]{3,2,1,0:T(8,128)} %get-tuple-element.87), channel_id=1, source_target_pairs={{0,12},{4,0},{8,4},{12,8},{1,13},{5,1},{9,5},{13,9},{2,14},{6,2},{... | collective-permute-start | bytes 2359304 | tf_op jit(solution)/shard_map/ppermute | solution.py:280
  88.0 105.6 %copy-start.9 = (f32[3,12,8,512]{3,2,1,0:T(8,128)}, f32[3,12,8,512]{3,2,1,0:T(8,128)S(1)}, u32[]{:S(2)}) copy-start(f32[3,12,8,512]{3,2,1,0:T(8,128)S(1)} %collective-permute-done.11.refs_11_.refs_9_) | copy-start | bytes 1769476
  88.0 144.1 %copy-start.10 = (f32[3,12,8,512]{3,2,1,0:T(8,128)}, f32[3,12,8,512]{3,2,1,0:T(8,128)S(1)}, u32[]{:S(2)}) copy-start(f32[3,12,8,512]{3,2,1,0:T(8,128)S(1)} %collective-permute-done.13.refs_14_.refs_12_) | copy-start | bytes 1769476
  88.0 104.5 %collective-permute-start.15 = (f32[12,4,8,512]{3,2,1,0:T(8,128)}, f32[12,4,8,512]{3,2,1,0:T(8,128)S(1)}, u32[]{:S(2)}, u32[]{:S(2)}) collective-permute-start(f32[12,4,8,512]{3,2,1,0:T(8,128)} %get-tuple-element.99), channel_id=1, source_target_pairs={{0,4},{4,8},{8,12},{12,0},{1,5},{5,9},{9,13},{13,1},{2,6},{6,10},{... | collective-permute-start | bytes 2359304 | tf_op jit(solution)/shard_map/ppermute | solution.py:280
  122.3 109.8 %collective-permute-start.16 = (f32[12,4,8,512]{3,2,1,0:T(8,128)}, f32[12,4,8,512]{3,2,1,0:T(8,128)S(1)}, u32[]{:S(2)}, u32[]{:S(2)}) collective-permute-start(f32[12,4,8,512]{3,2,1,0:T(8,128)} %get-tuple-element.100), channel_id=1, source_target_pairs={{0,8},{4,12},{8,0},{12,4},{1,9},{5,13},{9,1},{13,5},{2,10},{6,14},... | collective-permute-start | bytes 2359304 | tf_op jit(solution)/shard_map/ppermute | solution.py:280
  122.3 109.8 %copy-start.14 = (f32[12,4,8,512]{3,2,1,0:T(8,128)}, f32[12,4,8,512]{3,2,1,0:T(8,128)S(1)}, u32[]{:S(2)}) copy-start(f32[12,4,8,512]{3,2,1,0:T(8,128)S(1)} %collective-permute-done.10.refs_9_.refs_7_) | copy-start | bytes 2359300
  122.3 109.8 %collective-permute-start.17 = (f32[12,4,8,512]{3,2,1,0:T(8,128)}, f32[12,4,8,512]{3,2,1,0:T(8,128)S(1)}, u32[]{:S(2)}, u32[]{:S(2)}) collective-permute-start(f32[12,4,8,512]{3,2,1,0:T(8,128)} %get-tuple-element.101), channel_id=1, source_target_pairs={{0,12},{4,0},{8,4},{12,8},{1,13},{5,1},{9,5},{13,9},{2,14},{6,2},{... | collective-permute-start | bytes 2359304 | tf_op jit(solution)/shard_map/ppermute | solution.py:280
  172.4 59.8 %copy-start.15 = (f32[12,4,8,512]{3,2,1,0:T(8,128)}, f32[12,4,8,512]{3,2,1,0:T(8,128)S(1)}, u32[]{:S(2)}) copy-start(f32[12,4,8,512]{3,2,1,0:T(8,128)S(1)} %collective-permute-done.12.refs_12_.refs_10_) | copy-start | bytes 2359300
  172.4 59.8 %copy-start.16 = (f32[12,4,8,512]{3,2,1,0:T(8,128)}, f32[12,4,8,512]{3,2,1,0:T(8,128)S(1)}, u32[]{:S(2)}) copy-start(f32[12,4,8,512]{3,2,1,0:T(8,128)S(1)} %collective-permute-done.14.refs_15_.refs_13_) | copy-start | bytes 2359300
  172.4 136.9 %collective-permute-start.21 = (f32[12,3,8,512]{3,2,1,0:T(8,128)S(1)}, f32[12,3,8,512]{3,2,1,0:T(8,128)S(1)}, u32[]{:S(2)}, u32[]{:S(2)}) collective-permute-start(f32[12,3,8,512]{3,2,1,0:T(8,128)S(1)} %get-tuple-element.115), channel_id=1, source_target_pairs={{0,4},{4,8},{8,12},{12,0},{1,5},{5,9},{9,13},{13,1},{2,6},{6,10},{... | collective-permute-start | bytes 1769480 | tf_op jit(solution)/shard_map/ppermute | solution.py:280
  190.6 126.4 %collective-permute-start.22 = (f32[12,3,8,512]{3,2,1,0:T(8,128)S(1)}, f32[12,3,8,512]{3,2,1,0:T(8,128)}, u32[]{:S(2)}, u32[]{:S(2)}) collective-permute-start(f32[12,3,8,512]{3,2,1,0:T(8,128)S(1)} %get-tuple-element.116), channel_id=1, source_target_pairs={{0,8},{4,12},{8,0},{12,4},{1,9},{5,13},{9,1},{13,5},{2,10},{6,14},... | collective-permute-start | bytes 1769480 | tf_op jit(solution)/shard_map/ppermute | solution.py:280
  192.6 39.6 %copy-start.18 = (f32[12,4,8,512]{3,2,1,0:T(8,128)}, f32[12,4,8,512]{3,2,1,0:T(8,128)S(1)}, u32[]{:S(2)}) copy-start(f32[12,4,8,512]{3,2,1,0:T(8,128)S(1)} %collective-permute-done.15.refs_7_) | copy-start | bytes 2359300
  192.6 124.4 %collective-permute-start.23 = (f32[12,3,8,512]{3,2,1,0:T(8,128)S(1)}, f32[12,3,8,512]{3,2,1,0:T(8,128)}, u32[]{:S(2)}, u32[]{:S(2)}) collective-permute-start(f32[12,3,8,512]{3,2,1,0:T(8,128)S(1)} %get-tuple-element.117), channel_id=1, source_target_pairs={{0,12},{4,0},{8,4},{12,8},{1,13},{5,1},{9,5},{13,9},{2,14},{6,2},{... | collective-permute-start | bytes 1769480 | tf_op jit(solution)/shard_map/ppermute | solution.py:280
  232.1 0.9 copy-start.19
  232.1 1.1 copy-start.20
  288.7 34.8 %collective-permute-start.18 = (f32[12,1,8,512]{3,2,1,0:T(8,128)S(1)}, f32[12,1,8,512]{3,2,1,0:T(8,128)S(1)}, u32[]{:S(2)}, u32[]{:S(2)}) collective-permute-start(f32[12,1,8,512]{3,2,1,0:T(8,128)S(1)} %get-tuple-element.107), channel_id=1, source_target_pairs={{0,4},{4,8},{8,12},{12,0},{1,5},{5,9},{9,13},{13,1},{2,6},{6,10},{... | collective-permute-start | bytes 589832 | tf_op jit(solution)/shard_map/ppermute | solution.py:280
  306.0 17.5 %collective-permute-start.19 = (f32[12,1,8,512]{3,2,1,0:T(8,128)S(1)}, f32[12,1,8,512]{3,2,1,0:T(8,128)S(1)}, u32[]{:S(2)}, u32[]{:S(2)}) collective-permute-start(f32[12,1,8,512]{3,2,1,0:T(8,128)S(1)} %get-tuple-element.108), channel_id=1, source_target_pairs={{0,8},{4,12},{8,0},{12,4},{1,9},{5,13},{9,1},{13,5},{2,10},{6,14},... | collective-permute-start | bytes 589832 | tf_op jit(solution)/shard_map/ppermute | solution.py:280
  309.3 7.7 %copy-start.21 = (f32[12,3,8,512]{3,2,1,0:T(8,128)}, f32[12,3,8,512]{3,2,1,0:T(8,128)S(1)}, u32[]{:S(2)}) copy-start(f32[12,3,8,512]{3,2,1,0:T(8,128)S(1)} %collective-permute-done.21.refs_7_) | copy-start | bytes 1769476
  309.3 14.2 %collective-permute-start.20 = (f32[12,1,8,512]{3,2,1,0:T(8,128)S(1)}, f32[12,1,8,512]{3,2,1,0:T(8,128)S(1)}, u32[]{:S(2)}, u32[]{:S(2)}) collective-permute-start(f32[12,1,8,512]{3,2,1,0:T(8,128)S(1)} %get-tuple-element.109), channel_id=1, source_target_pairs={{0,12},{4,0},{8,4},{12,8},{1,13},{5,1},{9,5},{13,9},{2,14},{6,2},{... | collective-permute-start | bytes 589832 | tf_op jit(solution)/shard_map/ppermute | solution.py:280
  323.5 0.7 copy-start.22
  323.5 0.7 copy-start.23
  324.2 0.7 copy-start.24
